TPU v7x, 32 devices: a whole 2x2x4 slice. The times are simulated.
32 devices in a mesh: dp: 8 (over z, y), seq: 4 (over x, core).
Axes of the slice: x: 2, y: 2, z: 4, core: 2. Of those that a mesh axis runs over, the one named last changes fastest.
Arguments:
- residual: float32 [8192, 768], P(('dp', 'seq')), may hold values from -6 to 6
- cotangent: float32 [8192, 768], P(('dp', 'seq')), may hold values from -6 to 6
- segments: int32 [8192], P('dp'), may hold values from 0 to 15, as said below
- triple_weight: float32 [2, 768, 2304], P(None, 'dp', 'seq'), may hold values from -0.21875 to 0.21875
- triple_moment: float32 [2, 768, 2304], P(None, 'dp', 'seq'), may hold values from -0.33 to 0.33
- triple_square: float32 [2, 768, 2304], P(None, 'dp', 'seq'), may hold values from 0.00025 to 0.001
- triple_shadow: float32 [2, 768, 2304], P(None, 'dp', 'seq'), may hold values from -0.21875 to 0.21875
- output_weight: float32 [2, 768, 768], P(None, 'dp', 'seq'), may hold values from -0.875 to 0.875
- output_moment: float32 [2, 768, 768], P(None, 'dp', 'seq'), may hold values from -0.33 to 0.33
- output_square: float32 [2, 768, 768], P(None, 'dp', 'seq'), may hold values from 0.00025 to 0.001
- output_shadow: float32 [2, 768, 768], P(None, 'dp', 'seq'), may hold values from -0.875 to 0.875
- expand_weight: float32 [2, 768, 3072], P(None, 'dp', 'seq'), may hold values from -0.21875 to 0.21875
- expand_moment: float32 [2, 768, 3072], P(None, 'dp', 'seq'), may hold values from -0.33 to 0.33
- expand_square: float32 [2, 768, 3072], P(None, 'dp', 'seq'), may hold values from 0.00025 to 0.001
- expand_shadow: float32 [2, 768, 3072], P(None, 'dp', 'seq'), may hold values from -0.21875 to 0.21875
- shrink_weight: float32 [2, 3072, 768], P(None, 'dp', 'seq'), may hold values from -0.109375 to 0.109375
- shrink_moment: float32 [2, 3072, 768], P(None, 'dp', 'seq'), may hold values from -0.33 to 0.33
- shrink_square: float32 [2, 3072, 768], P(None, 'dp', 'seq'), may hold values from 0.00025 to 0.001
- shrink_shadow: float32 [2, 3072, 768], P(None, 'dp', 'seq'), may hold values from -0.109375 to 0.109375
- scales_weight: float32 [2, 4, 768], P(None, 'seq', 'dp'), may hold values from -0.5 to 2.3
- scales_moment: float32 [2, 4, 768], P(None, 'seq', 'dp'), may hold values from -0.33 to 0.33
- scales_square: float32 [2, 4, 768], P(None, 'seq', 'dp'), may hold values from 0.00025 to 0.32
- scales_shadow: float32 [2, 4, 768], P(None, 'seq', 'dp'), may hold values from -0.5 to 2.3
Outputs:
- block_out: float32 [8192, 768], P(('dp', 'seq'))
- input_grad: float32 [8192, 768], P(('dp', 'seq'))
- grad_norm: float32 [], replicated
- triple_updated: float32 [2, 768, 2304], P(None, 'dp', 'seq')
- triple_momentum: float32 [2, 768, 2304], P(None, 'dp', 'seq')
- triple_variance: float32 [2, 768, 2304], P(None, 'dp', 'seq')
- triple_average: float32 [2, 768, 2304], P(None, 'dp', 'seq')
- output_updated: float32 [2, 768, 768], P(None, 'dp', 'seq')
- output_momentum: float32 [2, 768, 768], P(None, 'dp', 'seq')
- output_variance: float32 [2, 768, 768], P(None, 'dp', 'seq')
- output_average: float32 [2, 768, 768], P(None, 'dp', 'seq')
- expand_updated: float32 [2, 768, 3072], P(None, 'dp', 'seq')
- expand_momentum: float32 [2, 768, 3072], P(None, 'dp', 'seq')
- expand_variance: float32 [2, 768, 3072], P(None, 'dp', 'seq')
- expand_average: float32 [2, 768, 3072], P(None, 'dp', 'seq')
- shrink_updated: float32 [2, 3072, 768], P(None, 'dp', 'seq')
- shrink_momentum: float32 [2, 3072, 768], P(None, 'dp', 'seq')
- shrink_variance: float32 [2, 3072, 768], P(None, 'dp', 'seq')
- shrink_average: float32 [2, 3072, 768], P(None, 'dp', 'seq')
- scales_updated: float32 [2, 4, 768], P(None, 'seq', 'dp')
- scales_momentum: float32 [2, 4, 768], P(None, 'seq', 'dp')
- scales_variance: float32 [2, 4, 768], P(None, 'seq', 'dp')
- scales_average: float32 [2, 4, 768], P(None, 'seq', 'dp')
Inputs may be any that keep to these rules, and one draw needn't show every extreme that they name: Ids never fall along the tokens; each aligned block of 1024 tokens holds whole segments only, and ids of different blocks differ; every segment has 1024 or half of 1024 tokens and starts at a multiple of half of 1024 within its block; ids need not be consecutive.
All inputs are finite; a program needn't handle non-finite values.
Results may differ from a plain program's by a relative error of at most 0.02.
Values may be sent and summed in bfloat16 or wider, within the bound.
A program may use at most 192 MiB of HBM per device.

v0:
```python
import math

import jax
import jax.numpy as jnp
from jax import lax
from jax.sharding import PartitionSpec as P

D = 768
FF = 3072
HD = 64
LAYERS = 2
STEP = 2


EPSILON = 1e-05
ROTARY_BASE = 10000.0
BETA_ONE = 0.9
BETA_TWO = 0.999
ADAM_EPSILON = 1e-08
DECAY_RATE = 0.01
SHADOW_RATE = 0.99
CLIP_RATIO = 0.5
RATE_FACTOR = 1.5
SCALES_RATE = 0.6
MASKED = -1000000000.0


def layer_norm(values, gain_row, shift_row):
    center = values - jnp.mean(values, axis=-1, keepdims=True)
    spread = jnp.mean(center * center, axis=-1, keepdims=True)
    return center * lax.rsqrt(spread + EPSILON) * gain_row + shift_row


def rotary(values, positions):
    row_count = values.shape[0]
    shaped = values.reshape(row_count, -1, HD)
    half_width = HD // 2
    inverse = 1.0 / ROTARY_BASE ** (jnp.arange(half_width, dtype=jnp.float32) * (2.0 / HD))
    angles = positions.astype(jnp.float32)[:, None] * inverse[None, :]
    cosine = jnp.cos(angles)[:, None, :]
    sine_table = jnp.sin(angles)[:, None, :]
    first_half = shaped[:, :, :half_width]
    second_half = shaped[:, :, half_width:]
    turned = jnp.concatenate(
        [
            first_half * cosine - second_half * sine_table,
            second_half * cosine + first_half * sine_table,
        ],
        axis=-1,
    )
    return turned.reshape(row_count, -1)


def over_rows(left_side, right_side):
    return lax.dot_general(
        left_side, right_side, (((0,), (0,)), ((), ())), preferred_element_type=jnp.float32
    )


def against(left_side, right_side):
    return lax.dot_general(
        left_side, right_side, (((1,), (1,)), ((), ())), preferred_element_type=jnp.float32
    )


def adam_step(weight, moment, square, shadow, gradient, step_rate):
    shadow_decay = min(SHADOW_RATE, (1.0 + STEP) / (10.0 + STEP))
    momentum = BETA_ONE * moment + (1.0 - BETA_ONE) * gradient
    variance = BETA_TWO * square + (1.0 - BETA_TWO) * gradient * gradient
    corrected = (
        momentum
        / (1.0 - BETA_ONE**STEP)
        / (jnp.sqrt(variance / (1.0 - BETA_TWO**STEP)) + ADAM_EPSILON)
    )
    updated = weight - step_rate * (corrected + DECAY_RATE * weight)
    average = shadow_decay * shadow + (1.0 - shadow_decay) * updated
    return (updated, momentum, variance, average)


def positions_here(segments, tokens_local):
    offset = lax.axis_index("seq") * tokens_local
    own_ids = lax.dynamic_slice_in_dim(segments, offset, tokens_local)
    earlier = (segments[None, :] < own_ids[:, None]).astype(jnp.int32)
    return offset + jnp.arange(tokens_local, dtype=jnp.int32) - jnp.sum(earlier, axis=1)


def attend_forward(queries, keys, values, segments):
    group_rows = queries.shape[0]
    block_rows = min(512, group_rows)
    block_count = group_rows // block_rows
    factor = HD ** (-0.5)
    key_heads = keys.reshape(group_rows, -1, HD)
    value_heads = values.reshape(group_rows, -1, HD)

    def one_block(packed):
        query_block, segment_block = packed
        query_heads = query_block.reshape(block_rows, -1, HD)
        scores = (
            jnp.einsum("qhd,khd->hqk", query_heads, key_heads, preferred_element_type=jnp.float32)
            * factor
        )
        same_doc = segment_block[:, None] == segments[None, :]
        scores = jnp.where(same_doc[None], scores, MASKED)
        maximum = jnp.max(scores, axis=-1, keepdims=True)
        exponent = jnp.exp(scores - maximum)
        row_total = jnp.sum(exponent, axis=-1, keepdims=True)
        weights = (exponent / row_total).astype(jnp.bfloat16)
        context = jnp.einsum(
            "hqk,khd->qhd", weights, value_heads, preferred_element_type=jnp.float32
        )
        return (
            context.reshape(block_rows, -1).astype(jnp.bfloat16),
            (maximum + jnp.log(row_total))[:, :, 0],
        )

    contexts, logsums = lax.map(
        one_block,
        (queries.reshape(block_count, block_rows, -1), segments.reshape(block_count, block_rows)),
    )
    return (contexts.reshape(group_rows, -1), logsums)


def attend_backward(queries, keys, values, segments, logsums, context_grad):
    group_rows = queries.shape[0]
    block_rows = min(512, group_rows)
    block_count = group_rows // block_rows
    factor = HD ** (-0.5)
    key_heads = keys.reshape(group_rows, -1, HD)
    value_heads = values.reshape(group_rows, -1, HD)

    def one_block(carry, packed):
        key_sum, value_sum = carry
        query_block, segment_block, logsum_block, grad_block = packed
        query_heads = query_block.reshape(block_rows, -1, HD)
        grad_heads = grad_block.reshape(block_rows, -1, HD)
        scores = (
            jnp.einsum("qhd,khd->hqk", query_heads, key_heads, preferred_element_type=jnp.float32)
            * factor
        )
        same_doc = segment_block[:, None] == segments[None, :]
        scores = jnp.where(same_doc[None], scores, MASKED)
        probs = jnp.exp(scores - logsum_block[:, :, None])
        value_sum = value_sum + jnp.einsum(
            "hqk,qhd->khd",
            probs.astype(jnp.bfloat16),
            grad_heads,
            preferred_element_type=jnp.float32,
        )
        probs_grad = jnp.einsum(
            "qhd,khd->hqk", grad_heads, value_heads, preferred_element_type=jnp.float32
        )
        row_dot = jnp.sum(probs * probs_grad, axis=-1, keepdims=True)
        score_grad = (probs * (probs_grad - row_dot)).astype(jnp.bfloat16)
        query_part = (
            jnp.einsum("hqk,khd->qhd", score_grad, key_heads, preferred_element_type=jnp.float32)
            * factor
        )
        key_sum = key_sum + jnp.einsum(
            "hqk,qhd->khd", score_grad, query_heads, preferred_element_type=jnp.float32
        )
        return ((key_sum, value_sum), query_part.reshape(block_rows, -1).astype(jnp.bfloat16))

    zeros_start = jnp.zeros(key_heads.shape, jnp.float32)
    carried, query_parts = lax.scan(
        one_block,
        (zeros_start, zeros_start),
        (
            queries.reshape(block_count, block_rows, -1),
            segments.reshape(block_count, block_rows),
            logsums,
            context_grad.reshape(block_count, block_rows, -1),
        ),
    )
    key_grad = (carried[0] * factor).reshape(group_rows, -1).astype(jnp.bfloat16)
    value_grad = carried[1].reshape(group_rows, -1).astype(jnp.bfloat16)
    return (query_parts.reshape(group_rows, -1), key_grad, value_grad)


def forward_layer(stream, weights, positions, segments):
    triple, output, expand, shrink, scales = weights
    scale_rows = scales.astype(jnp.float32)
    width = stream.shape[1]
    normed_first = layer_norm(stream, scale_rows[0], scale_rows[1]).astype(jnp.bfloat16)
    projected = jnp.dot(normed_first, triple, preferred_element_type=jnp.float32)
    queries = rotary(projected[:, :width], positions).astype(jnp.bfloat16)
    keys = rotary(projected[:, width : 2 * width], positions).astype(jnp.bfloat16)
    values = projected[:, 2 * width :].astype(jnp.bfloat16)
    head_parts = (
        lax.all_to_all(queries, "seq", split_axis=1, concat_axis=0, tiled=True),
        lax.all_to_all(keys, "seq", split_axis=1, concat_axis=0, tiled=True),
        lax.all_to_all(values, "seq", split_axis=1, concat_axis=0, tiled=True),
    )
    context_heads, logsums = attend_forward(head_parts[0], head_parts[1], head_parts[2], segments)
    context = lax.all_to_all(context_heads, "seq", split_axis=0, concat_axis=1, tiled=True)
    middle = stream + jnp.dot(context, output, preferred_element_type=jnp.float32)
    normed_second = layer_norm(middle, scale_rows[2], scale_rows[3]).astype(jnp.bfloat16)
    hidden = jnp.dot(normed_second, expand, preferred_element_type=jnp.float32)
    active = jax.nn.gelu(hidden, approximate=False).astype(jnp.bfloat16)
    result = middle + jnp.dot(active, shrink, preferred_element_type=jnp.float32)
    saved = (
        stream,
        normed_first,
        head_parts[0],
        head_parts[1],
        head_parts[2],
        logsums,
        context,
        middle,
        normed_second,
        hidden,
        active,
    )
    return (result, saved)


def backward_layer(grad_out, weights, saved, positions, segments):
    triple, output, expand, shrink, scales = weights
    scale_rows = scales.astype(jnp.float32)
    (
        stream,
        normed_first,
        queries,
        keys,
        values,
        logsums,
        context,
        middle,
        normed_second,
        hidden,
        active,
    ) = saved
    grad_low = grad_out.astype(jnp.bfloat16)
    shrink_grad = over_rows(active, grad_low)
    active_grad = against(grad_low, shrink)
    gelu_pull = jax.vjp(lambda inputs: jax.nn.gelu(inputs, approximate=False), hidden)[1]
    hidden_grad = gelu_pull(active_grad)[0].astype(jnp.bfloat16)
    expand_grad = over_rows(normed_second, hidden_grad)
    normed_second_grad = against(hidden_grad, expand)
    second_pull = jax.vjp(layer_norm, middle, scale_rows[2], scale_rows[3])[1]
    middle_part, gain_second, shift_second = second_pull(normed_second_grad)
    middle_grad = grad_out + middle_part
    middle_low = middle_grad.astype(jnp.bfloat16)
    output_grad = over_rows(context, middle_low)
    context_grad = against(middle_low, output).astype(jnp.bfloat16)
    context_heads = lax.all_to_all(context_grad, "seq", split_axis=1, concat_axis=0, tiled=True)
    query_grad, key_grad, value_grad = attend_backward(
        queries, keys, values, segments, logsums, context_heads
    )
    token_parts = (
        lax.all_to_all(query_grad, "seq", split_axis=0, concat_axis=1, tiled=True),
        lax.all_to_all(key_grad, "seq", split_axis=0, concat_axis=1, tiled=True),
        lax.all_to_all(value_grad, "seq", split_axis=0, concat_axis=1, tiled=True),
    )
    projected_grad = jnp.concatenate(
        [
            rotary(token_parts[0].astype(jnp.float32), -positions),
            rotary(token_parts[1].astype(jnp.float32), -positions),
            token_parts[2].astype(jnp.float32),
        ],
        axis=1,
    ).astype(jnp.bfloat16)
    triple_grad = over_rows(normed_first, projected_grad)
    normed_first_grad = against(projected_grad, triple)
    first_pull = jax.vjp(layer_norm, stream, scale_rows[0], scale_rows[1])[1]
    stream_part, gain_first, shift_first = first_pull(normed_first_grad)
    scales_grad = jnp.stack([gain_first, shift_first, gain_second, shift_second])
    shares = (
        lax.psum_scatter(triple_grad, "dp", scatter_dimension=0, tiled=True),
        lax.psum_scatter(output_grad, "dp", scatter_dimension=0, tiled=True),
        lax.psum_scatter(expand_grad, "dp", scatter_dimension=0, tiled=True),
        lax.psum_scatter(shrink_grad, "dp", scatter_dimension=0, tiled=True),
        lax.psum_scatter(scales_grad, "dp", scatter_dimension=1, tiled=True),
    )
    owned = (
        lax.psum_scatter(
            shares[0].astype(jnp.bfloat16), "seq", scatter_dimension=1, tiled=True
        ).astype(jnp.float32),
        lax.psum_scatter(
            shares[1].astype(jnp.bfloat16), "seq", scatter_dimension=1, tiled=True
        ).astype(jnp.float32),
        lax.psum_scatter(
            shares[2].astype(jnp.bfloat16), "seq", scatter_dimension=1, tiled=True
        ).astype(jnp.float32),
        lax.psum_scatter(
            shares[3].astype(jnp.bfloat16), "seq", scatter_dimension=1, tiled=True
        ).astype(jnp.float32),
        lax.psum_scatter(
            shares[4].astype(jnp.bfloat16), "seq", scatter_dimension=0, tiled=True
        ).astype(jnp.float32),
    )
    return (middle_grad + stream_part, owned)


def local(
    residual,
    cotangent,
    segments,
    triple_weight,
    triple_moment,
    triple_square,
    triple_shadow,
    output_weight,
    output_moment,
    output_square,
    output_shadow,
    expand_weight,
    expand_moment,
    expand_square,
    expand_shadow,
    shrink_weight,
    shrink_moment,
    shrink_square,
    shrink_shadow,
    scales_weight,
    scales_moment,
    scales_square,
    scales_shadow,
):
    tokens_local = residual.shape[0]
    positions = positions_here(segments, tokens_local)
    fetched = []
    kept = []
    stream = residual
    for layer_index in range(LAYERS):
        weights = (
            lax.all_gather(
                lax.all_gather(
                    triple_weight[layer_index].astype(jnp.bfloat16), "seq", axis=1, tiled=True
                ),
                "dp",
                axis=0,
                tiled=True,
            ),
            lax.all_gather(
                lax.all_gather(
                    output_weight[layer_index].astype(jnp.bfloat16), "seq", axis=1, tiled=True
                ),
                "dp",
                axis=0,
                tiled=True,
            ),
            lax.all_gather(
                lax.all_gather(
                    expand_weight[layer_index].astype(jnp.bfloat16), "seq", axis=1, tiled=True
                ),
                "dp",
                axis=0,
                tiled=True,
            ),
            lax.all_gather(
                lax.all_gather(
                    shrink_weight[layer_index].astype(jnp.bfloat16), "seq", axis=1, tiled=True
                ),
                "dp",
                axis=0,
                tiled=True,
            ),
            lax.all_gather(
                lax.all_gather(
                    scales_weight[layer_index].astype(jnp.bfloat16), "seq", axis=0, tiled=True
                ),
                "dp",
                axis=1,
                tiled=True,
            ),
        )
        fetched.append(weights)
        stream, saved = forward_layer(stream, weights, positions, segments)
        kept.append(saved)
    gradient_shards = []
    partials = []
    grad_stream = cotangent
    for layer_index in reversed(range(LAYERS)):
        weights = (
            lax.all_gather(
                lax.all_gather(
                    triple_weight[layer_index].astype(jnp.bfloat16), "seq", axis=1, tiled=True
                ),
                "dp",
                axis=0,
                tiled=True,
            ),
            lax.all_gather(
                lax.all_gather(
                    output_weight[layer_index].astype(jnp.bfloat16), "seq", axis=1, tiled=True
                ),
                "dp",
                axis=0,
                tiled=True,
            ),
            lax.all_gather(
                lax.all_gather(
                    expand_weight[layer_index].astype(jnp.bfloat16), "seq", axis=1, tiled=True
                ),
                "dp",
                axis=0,
                tiled=True,
            ),
            lax.all_gather(
                lax.all_gather(
                    shrink_weight[layer_index].astype(jnp.bfloat16), "seq", axis=1, tiled=True
                ),
                "dp",
                axis=0,
                tiled=True,
            ),
            lax.all_gather(
                lax.all_gather(
                    scales_weight[layer_index].astype(jnp.bfloat16), "seq", axis=0, tiled=True
                ),
                "dp",
                axis=1,
                tiled=True,
            ),
        )
        grad_stream, owned = backward_layer(
            grad_stream, weights, kept[layer_index], positions, segments
        )
        gradient_shards.insert(0, owned)
        local_squares = (
            jnp.sum(owned[0] * owned[0])
            + jnp.sum(owned[1] * owned[1])
            + jnp.sum(owned[2] * owned[2])
            + jnp.sum(owned[3] * owned[3])
            + jnp.sum(owned[4] * owned[4])
        )
        partials.append(local_squares)
    squares = partials[0]
    for extra_part in partials[1:]:
        squares = squares + extra_part
    squares = lax.psum(squares, ("dp", "seq"))
    grad_norm = jnp.sqrt(squares)
    limit = CLIP_RATIO * math.sqrt(float(LAYERS * (4 * D * D + 2 * D * FF + 4 * D)))
    factor = limit / (grad_norm + 1e-06)

    def stacked(kind_index):
        return (
            jnp.stack([gradient_shards[layer_index][kind_index] for layer_index in range(LAYERS)])
            * factor
        )

    triple_updated, triple_momentum, triple_variance, triple_average = adam_step(
        triple_weight,
        triple_moment,
        triple_square,
        triple_shadow,
        stacked(0),
        RATE_FACTOR / math.sqrt(D),
    )
    output_updated, output_momentum, output_variance, output_average = adam_step(
        output_weight,
        output_moment,
        output_square,
        output_shadow,
        stacked(1),
        RATE_FACTOR / math.sqrt(D // 16),
    )
    expand_updated, expand_momentum, expand_variance, expand_average = adam_step(
        expand_weight,
        expand_moment,
        expand_square,
        expand_shadow,
        stacked(2),
        RATE_FACTOR / math.sqrt(D),
    )
    shrink_updated, shrink_momentum, shrink_variance, shrink_average = adam_step(
        shrink_weight,
        shrink_moment,
        shrink_square,
        shrink_shadow,
        stacked(3),
        RATE_FACTOR / math.sqrt(FF),
    )
    scales_updated, scales_momentum, scales_variance, scales_average = adam_step(
        scales_weight, scales_moment, scales_square, scales_shadow, stacked(4), SCALES_RATE
    )
    return (
        stream,
        grad_stream,
        grad_norm,
        triple_updated,
        triple_momentum,
        triple_variance,
        triple_average,
        output_updated,
        output_momentum,
        output_variance,
        output_average,
        expand_updated,
        expand_momentum,
        expand_variance,
        expand_average,
        shrink_updated,
        shrink_momentum,
        shrink_variance,
        shrink_average,
        scales_updated,
        scales_momentum,
        scales_variance,
        scales_average,
    )


def solution(mesh):
    return jax.shard_map(
        local,
        mesh=mesh,
        in_specs=(
            P(("dp", "seq"), None),
            P(("dp", "seq"), None),
            P("dp"),
            P(None, "dp", "seq"),
            P(None, "dp", "seq"),
            P(None, "dp", "seq"),
            P(None, "dp", "seq"),
            P(None, "dp", "seq"),
            P(None, "dp", "seq"),
            P(None, "dp", "seq"),
            P(None, "dp", "seq"),
            P(None, "dp", "seq"),
            P(None, "dp", "seq"),
            P(None, "dp", "seq"),
            P(None, "dp", "seq"),
            P(None, "dp", "seq"),
            P(None, "dp", "seq"),
            P(None, "dp", "seq"),
            P(None, "dp", "seq"),
            P(None, "seq", "dp"),
            P(None, "seq", "dp"),
            P(None, "seq", "dp"),
            P(None, "seq", "dp"),
        ),
        out_specs=(
            P(("dp", "seq"), None),
            P(("dp", "seq"), None),
            P(),
            P(None, "dp", "seq"),
            P(None, "dp", "seq"),
            P(None, "dp", "seq"),
            P(None, "dp", "seq"),
            P(None, "dp", "seq"),
            P(None, "dp", "seq"),
            P(None, "dp", "seq"),
            P(None, "dp", "seq"),
            P(None, "dp", "seq"),
            P(None, "dp", "seq"),
            P(None, "dp", "seq"),
            P(None, "dp", "seq"),
            P(None, "dp", "seq"),
            P(None, "dp", "seq"),
            P(None, "dp", "seq"),
            P(None, "dp", "seq"),
            P(None, "seq", "dp"),
            P(None, "seq", "dp"),
            P(None, "seq", "dp"),
            P(None, "seq", "dp"),
        ),
        check_vma=False,
    )
```

profile of v0, /device:TPU:0, one launch (start us, length us, event | category | flops | bytes accessed | tf_op | source)
XLA Modules:
  0.0 2101.7 jit_solution(5274115960357684858)
XLA Ops:
  9.0 12.2 all-gather.2
  75.8 32.1 %all-gather.1 = bf16[4,1,768]{0,1,2:T(2,128)(2,1)S(1)} all-gather(bf16[4,1,96]{0,1,2:T(2,128)(2,1)S(1)} %copy.286), channel_id=3, replica_groups=mesh['dp'=8,'seq'=4] {'dp'}, dimensions={2}, use_global_device_ids=true | all-gather | bytes 6912 | tf_op jit(solution)/shard_map/all_gather | solution.py:358
  108.3 10.9 slice_reduce_fusion.5
  159.4 11.6 all-gather.16
  175.9 16.8 while.54
  206.0 32.7 %all-gather.11 = bf16[4,1,768]{0,1,2:T(2,128)(2,1)S(1)} all-gather(bf16[4,1,96]{0,1,2:T(2,128)(2,1)S(1)} %copy.300), channel_id=13, replica_groups=mesh['dp'=8,'seq'=4] {'dp'}, dimensions={2}, use_global_device_ids=true | all-gather | bytes 6912 | tf_op jit(solution)/shard_map/all_gather | solution.py:358
  252.3 11.6 multiply_convert_fusion.3
  263.9 35.3 %all-gather.35.cloned.1.call-done = bf16[1,3072,768]{1,2,0:T(8,128)(2,1)} async-done(((bf16[1,384,768]{1,2,0:T(8,128)(2,1)}), bf16[1,3072,768]{1,2,0:T(8,128)(2,1)}) %all-gather.35.cloned.1.call-update) | async-done | bytes 4718608 | tf_op jit(solution)/shard_map/all_gather | solution.py:350
  303.8 61.4 %all-gather.37.cloned.1.call-done = bf16[1,768,2304]{2,1,0:T(8,128)(2,1)} async-done(((bf16[1,96,2304]{2,1,0:T(8,128)(2,1)}), bf16[1,768,2304]{2,1,0:T(8,128)(2,1)}) %all-gather.37.cloned.1.call-update) | async-done | bytes 3538960 | tf_op jit(solution)/shard_map/all_gather | solution.py:326
  403.4 11.8 all-gather.18
  420.2 17.0 while.55
  451.7 36.6 %all-gather.41.cloned.1.call-done = bf16[1,768,3072]{2,1,0:T(8,128)(2,1)} async-done(((bf16[1,96,3072]{2,1,0:T(8,128)(2,1)}), bf16[1,768,3072]{2,1,0:T(8,128)(2,1)}) %all-gather.41.cloned.1.call-update) | async-done | bytes 4718608 | tf_op jit(solution)/shard_map/all_gather | solution.py:342
  488.3 11.5 multiply_convert_fusion.2
  499.8 69.7 %all-gather.43.cloned.1.call-done = bf16[1,3072,768]{1,2,0:T(8,128)(2,1)} async-done(((bf16[1,384,768]{1,2,0:T(8,128)(2,1)}), bf16[1,3072,768]{1,2,0:T(8,128)(2,1)}) %all-gather.43.cloned.1.call-update) | async-done | bytes 4718608 | tf_op jit(solution)/shard_map/all_gather | solution.py:350
  594.5 36.0 %while.56 = (s32[]{:T(128)}, f32[1024,3,64]{0,2,1:T(8,128)}, f32[1024,3,64]{0,2,1:T(8,128)}, bf16[2,512,192]{1,2,0:T(8,128)(2,1)}, bf16[2,512,192]{1,2,0:T(8,128...) while((s32[]{:T(128)}, f32[1024,3,64]{0,2,1:T(8,128)}, ...), condition=%wide.region_21.22_spmd.clone, body=%wide.region_19.21_spmd.clone.sunk | while | flops 1031731712 | bytes 113758600 | solution.py:164
  699.6 36.3 %while.57 = (s32[]{:T(128)}, f32[1024,3,64]{0,2,1:T(8,128)}, f32[1024,3,64]{0,2,1:T(8,128)}, bf16[2,512,192]{1,2,0:T(8,128)(2,1)}, bf16[2,512,192]{1,2,0:T(8,128...) while((s32[]{:T(128)}, f32[1024,3,64]{0,2,1:T(8,128)}, ...), condition=%wide.region_28.29_spmd.clone, body=%wide.region_26.28_spmd.clone.sunk | while | flops 1031731712 | bytes 113758600 | solution.py:164
  812.9 109.7 %reduce-scatter.35.cloned.1.call-done = f32[96,2304]{1,0:T(8,128)} async-done(((f32[768,2304]{1,0:T(8,128)}), f32[96,2304]{1,0:T(8,128)}) %reduce-scatter.35.cloned.1.call-update) | async-done | bytes 884752 | tf_op jit(solution)/shard_map/reduce_scatter | solution.py:268
  931.5 123.1 %reduce-scatter.45.cloned.1.call-done = f32[96,2304]{1,0:T(8,128)} async-done(((f32[768,2304]{1,0:T(8,128)}), f32[96,2304]{1,0:T(8,128)}) %reduce-scatter.45.cloned.1.call-update) | async-done | bytes 884752 | tf_op jit(solution)/shard_map/reduce_scatter | solution.py:268
  1057.0 163.8 %reduce-scatter.39.cloned.1.call-done = f32[96,3072]{1,0:T(8,128)} async-done(((f32[768,3072]{1,0:T(8,128)}), f32[96,3072]{1,0:T(8,128)}) %reduce-scatter.39.cloned.1.call-update) | async-done | bytes 1179664 | tf_op jit(solution)/shard_map/reduce_scatter | solution.py:270
  1223.6 163.2 %reduce-scatter.43.cloned.1.call-done = f32[384,768]{1,0:T(8,128)} async-done(((f32[3072,768]{1,0:T(8,128)}), f32[384,768]{1,0:T(8,128)}) %reduce-scatter.43.cloned.1.call-update) | async-done | bytes 1179664 | tf_op jit(solution)/shard_map/reduce_scatter | solution.py:271
  1394.5 56.6 %reduce-scatter.61.cloned.1.call-done = f32[96,4]{1,0:T(8,128)} async-done(((f32[768,4]{1,0:T(8,128)}), f32[96,4]{1,0:T(8,128)}) %reduce-scatter.61.cloned.1.call-update) | async-done | bytes 1552
  1452.3 164.7 %reduce-scatter.49.cloned.1.call-done = f32[96,3072]{1,0:T(8,128)} async-done(((f32[768,3072]{1,0:T(8,128)}), f32[96,3072]{1,0:T(8,128)}) %reduce-scatter.49.cloned.1.call-update) | async-done | bytes 1179664 | tf_op jit(solution)/shard_map/reduce_scatter | solution.py:270
  1620.2 60.9 %reduce-scatter.69.cloned.1.call-done = f32[96,4]{1,0:T(8,128)} async-done(((f32[768,4]{1,0:T(8,128)}), f32[96,4]{1,0:T(8,128)}) %reduce-scatter.69.cloned.1.call-update) | async-done | bytes 1552
  1705.0 20.6 reduce-scatter.65.cloned.1.call-done
  1727.7 22.9 %reduce-scatter.55.cloned.1.call-done = bf16[576,96]{1,0:T(8,128)(2,1)} async-done(((bf16[2304,96]{1,0:T(8,128)(2,1)}), bf16[576,96]{1,0:T(8,128)(2,1)}) %reduce-scatter.55.cloned.1.call-update) | async-done | bytes 110608
  1753.7 164.0 %reduce-scatter.53.cloned.1.call-done = f32[384,768]{1,0:T(8,128)} async-done(((f32[3072,768]{1,0:T(8,128)}), f32[384,768]{1,0:T(8,128)}) %reduce-scatter.53.cloned.1.call-update) | async-done | bytes 1179664 | tf_op jit(solution)/shard_map/reduce_scatter | solution.py:271
  1920.1 21.8 %reduce-scatter.63.cloned.1.call-done = bf16[576,96]{1,0:T(8,128)(2,1)} async-done(((bf16[2304,96]{1,0:T(8,128)(2,1)}), bf16[576,96]{1,0:T(8,128)(2,1)}) %reduce-scatter.63.cloned.1.call-update) | async-done | bytes 110608
  1945.0 22.1 %reduce-scatter.41.cloned.1.call-done = bf16[96,768]{1,0:T(8,128)(2,1)} async-done(((bf16[96,3072]{1,0:T(8,128)(2,1)}), bf16[96,768]{1,0:T(8,128)(2,1)}) %reduce-scatter.41.cloned.1.call-update) | async-done | bytes 147472 | tf_op jit(solution)/shard_map/reduce_scatter | solution.py:281
  1969.4 22.8 %reduce-scatter.59.cloned.1.call-done = bf16[192,384]{1,0:T(8,128)(2,1)} async-done(((bf16[768,384]{1,0:T(8,128)(2,1)}), bf16[192,384]{1,0:T(8,128)(2,1)}) %reduce-scatter.59.cloned.1.call-update) | async-done | bytes 147472
  1996.0 21.3 %reduce-scatter.51.cloned.1.call-done = bf16[96,768]{1,0:T(8,128)(2,1)} async-done(((bf16[96,3072]{1,0:T(8,128)(2,1)}), bf16[96,768]{1,0:T(8,128)(2,1)}) %reduce-scatter.51.cloned.1.call-update) | async-done | bytes 147472 | tf_op jit(solution)/shard_map/reduce_scatter | solution.py:281
  2019.5 22.8 %reduce-scatter.67.cloned.1.call-done = bf16[192,384]{1,0:T(8,128)(2,1)} async-done(((bf16[768,384]{1,0:T(8,128)(2,1)}), bf16[192,384]{1,0:T(8,128)(2,1)}) %reduce-scatter.67.cloned.1.call-update) | async-done | bytes 147472
  2046.1 39.4 %psum.7 = f32[]{:T(128)} all-reduce(f32[]{:T(128)S(6)} %add.407), channel_id=1, replica_groups=mesh['dp'=8,'seq'=4] {'dp','seq'}, use_global_device_ids=true, to_apply=%region_69.70 | all-reduce | flops 1 | bytes 8 | tf_op jit(solution)/shard_map/psum | solution.py:431
  (704 shorter events, 539.2 us)
Async XLA Ops:
  7.2 113.7 %all-gather.29.cloned.1.call-start = ((), (), s32[]{:S(2)}) async-start(), calls=%async_computation.44 | async-start | bytes 3981312 | tf_op jit(solution)/shard_map/all_gather | solution.py:326
  23.5 226.5 %all-gather.31.cloned.1.call-start = ((), (), s32[]{:S(2)}) async-start(), calls=%async_computation.45 | async-start | bytes 1327104 | tf_op jit(solution)/shard_map/all_gather | solution.py:334
  31.4 220.9 %all-gather.33.cloned.1.call-start = ((), (), s32[]{:S(2)}) async-start(), calls=%async_computation.46 | async-start | bytes 5308416 | tf_op jit(solution)/shard_map/all_gather | solution.py:342
  40.3 258.9 %all-gather.35.cloned.1.call-start = ((), (), s32[]{:S(2)}) async-start(), calls=%async_computation.47 | async-start | bytes 5308416 | tf_op jit(solution)/shard_map/all_gather | solution.py:350
  49.3 315.9 %all-gather.37.cloned.1.call-start = ((), (), s32[]{:S(2)}) async-start(), calls=%async_computation.48 | async-start | bytes 3981312 | tf_op jit(solution)/shard_map/all_gather | solution.py:326
  62.5 379.5 %all-gather.39.cloned.1.call-start = ((), (), s32[]{:S(2)}) async-start(), calls=%async_computation.49 | async-start | bytes 1327104 | tf_op jit(solution)/shard_map/all_gather | solution.py:334
  144.0 11.6 all-to-all-start.1
  155.6 18.3 all-to-all-start.2
  159.1 329.2 %all-gather.41.cloned.1.call-start = ((), (), s32[]{:S(2)}) async-start(), calls=%async_computation.50 | async-start | bytes 5308416 | tf_op jit(solution)/shard_map/all_gather | solution.py:342
  194.1 55.9 %all-to-all-start.3 = ((bf16[4,256,192]{1,2,0:T(8,128)(2,1)}), bf16[4,256,192]{1,2,0:T(8,128)(2,1)S(1)}, u32[]{:S(2)}, u32[]{:S(2)}) async-start(bf16[4,256,192]{1,2,0:T(8,128)(2,1)} %copy.297), calls=%async_computation.3 | async-start | bytes 786432 | tf_op jit(solution)/shard_map/all_to_all | solution.py:194
  388.2 11.6 all-to-all-start.5
  399.9 18.3 all-to-all-start.6
  403.3 166.2 %all-gather.43.cloned.1.call-start = ((), (), s32[]{:S(2)}) async-start(), calls=%async_computation.51 | async-start | bytes 5308416 | tf_op jit(solution)/shard_map/all_gather | solution.py:350
  581.1 11.3 all-to-all-start.8
  647.3 161.8 %reduce-scatter.37.cloned.1.call-start = ((), (), s32[]{:S(2)}) async-start(), calls=%async_computation.35 | async-start | bytes 2654208 | tf_op jit(solution)/shard_map/reduce_scatter | solution.py:269
  658.2 152.8 %reduce-scatter.47.cloned.1.call-start = ((), (), s32[]{:S(2)}) async-start(), calls=%async_computation.40 | async-start | bytes 2654208 | tf_op jit(solution)/shard_map/reduce_scatter | solution.py:269
  679.5 243.1 %reduce-scatter.35.cloned.1.call-start = ((), (), s32[]{:S(2)}) async-start(), calls=%async_computation.34 | async-start | bytes 7962624 | tf_op jit(solution)/shard_map/reduce_scatter | solution.py:268
  763.6 291.0 %reduce-scatter.45.cloned.1.call-start = ((), (), s32[]{:S(2)}) async-start(), calls=%async_computation.39 | async-start | bytes 7962624 | tf_op jit(solution)/shard_map/reduce_scatter | solution.py:268
  775.2 445.6 %reduce-scatter.39.cloned.1.call-start = ((), (), s32[]{:S(2)}) async-start(), calls=%async_computation.36 | async-start | bytes 10616832 | tf_op jit(solution)/shard_map/reduce_scatter | solution.py:270
  783.1 603.7 %reduce-scatter.43.cloned.1.call-start = ((), (), s32[]{:S(2)}) async-start(), calls=%async_computation.38 | async-start | bytes 10616832 | tf_op jit(solution)/shard_map/reduce_scatter | solution.py:271
  790.7 660.3 %reduce-scatter.61.cloned.1.call-start = ((), (), s32[]{:S(2)}) async-start(), calls=%async_computation.55 | async-start | bytes 442368
  795.9 821.1 %reduce-scatter.49.cloned.1.call-start = ((), (), s32[]{:S(2)}) async-start(), calls=%async_computation.41 | async-start | bytes 10616832 | tf_op jit(solution)/shard_map/reduce_scatter | solution.py:270
  802.7 878.4 %reduce-scatter.69.cloned.1.call-start = ((), (), s32[]{:S(2)}) async-start(), calls=%async_computation.59 | async-start | bytes 442368
  809.1 893.7 %reduce-scatter.57.cloned.1.call-start = ((), (), s32[]{:S(2)}) async-start(), calls=%async_computation.53 | async-start | bytes 245760
  811.0 914.6 %reduce-scatter.65.cloned.1.call-start = ((), (), s32[]{:S(2)}) async-start(), calls=%async_computation.57 | async-start | bytes 245760
  812.9 937.7 %reduce-scatter.55.cloned.1.call-start = ((), (), s32[]{:S(2)}) async-start(), calls=%async_computation.52 | async-start | bytes 737280
  924.9 992.8 %reduce-scatter.53.cloned.1.call-start = ((), (), s32[]{:S(2)}) async-start(), calls=%async_computation.43 | async-start | bytes 10616832 | tf_op jit(solution)/shard_map/reduce_scatter | solution.py:271
  931.5 1010.5 %reduce-scatter.63.cloned.1.call-start = ((), (), s32[]{:S(2)}) async-start(), calls=%async_computation.56 | async-start | bytes 737280
  1057.0 910.2 %reduce-scatter.41.cloned.1.call-start = ((), (), s32[]{:S(2)}) async-start(), calls=%async_computation.37 | async-start | bytes 737280 | tf_op jit(solution)/shard_map/reduce_scatter | solution.py:281
  1223.0 769.2 %reduce-scatter.59.cloned.1.call-start = ((), (), s32[]{:S(2)}) async-start(), calls=%async_computation.54 | async-start | bytes 737280
  1389.3 628.0 %reduce-scatter.51.cloned.1.call-start = ((), (), s32[]{:S(2)}) async-start(), calls=%async_computation.42 | async-start | bytes 737280 | tf_op jit(solution)/shard_map/reduce_scatter | solution.py:281
  1619.1 423.2 %reduce-scatter.67.cloned.1.call-start = ((), (), s32[]{:S(2)}) async-start(), calls=%async_computation.58 | async-start | bytes 737280
  (166 other events, 4623.0 us)
Sparse Core Ops, SparseCore 0:
  23.6 68.1 all-gather.28
  94.6 39.3 all-gather.30
  136.2 79.6 all-gather.32
  217.8 81.2 all-gather.34
  301.8 63.3 all-gather.36
  367.8 39.5 all-gather.38
  409.6 78.6 all-gather.40
  490.3 79.1 all-gather.42
  651.6 67.6 reduce-scatter.36
  722.7 68.0 reduce-scatter.46
  794.5 128.0 reduce-scatter.34
  926.6 128.0 reduce-scatter.44
  1058.3 162.4 reduce-scatter.38
  1224.2 162.5 reduce-scatter.42
  1390.5 60.4 reduce-scatter.60
  1454.5 162.4 reduce-scatter.48
  1620.6 60.4 reduce-scatter.68
  1684.0 18.6 reduce-scatter.56
  1705.8 19.7 reduce-scatter.64
  1728.5 22.0 reduce-scatter.54
  1754.2 163.4 reduce-scatter.52
  1920.8 21.1 reduce-scatter.62
  1945.0 22.0 reduce-scatter.40
  1970.1 22.0 reduce-scatter.58
  1995.2 22.0 reduce-scatter.50
  2020.2 22.0 reduce-scatter.66
where the time goes:
time: 2110 us; the launch traced here: 2100 us
  waiting for transfers between devices  1450 us (69%)
  blocking collectives  199 us (9%)
  matrix products  173 us (8%)
  local copies, waits for them, and re-layouts  119 us (6%)
  other arithmetic  73.3 us (3%)
  starting transfers between devices  59.1 us (3%)
  between operations  24.7 us (1%)
    reduce_scatter x2, waiting for transfers between devices, backward_layer(): lax.psum_scatter(expand_grad, 'dp', scatter_dimension=0, tiled=True)  328 us
    reduce_scatter x2, waiting for transfers between devices, backward_layer(): lax.psum_scatter(shrink_grad, 'dp', scatter_dimension=0, tiled=True)  327 us
    unnamed x34, waiting for transfers between devices  240 us
    reduce_scatter x2, waiting for transfers between devices, backward_layer(): lax.psum_scatter(triple_grad, 'dp', scatter_dimension=0, tiled=True)  233 us
    all_gather x2, waiting for transfers between devices, local(): lax.all_gather(lax.all_gather(shrink_weight[layer_index].astype(jnp.bfloa...  105 us
    all_gather x2, blocking collectives, local(): lax.all_gather(lax.all_gather(scales_weight[layer_index].astype(jnp.bfloa...  64.8 us
    all_gather x2, waiting for transfers between devices, local(): lax.all_gather(lax.all_gather(triple_weight[layer_index].astype(jnp.bfloa...  61.4 us
    reduce_scatter x2, waiting for transfers between devices, backward_layer(): lax.psum_scatter(shares[2].astype(jnp.bfloat16), 'seq', scatter_dimension...  43.4 us
  transfers between devices with their start and end apart: 42, of which 33 were waited for; matrix products, arithmetic and copies ran while one was open for 14% of the time, Pallas kernels for 0%

commit v1 on v0

v1 whole, which is shorter than its diff:
```python
import functools
import math

import jax
import jax.numpy as jnp
from jax import lax
from jax.experimental import pallas as pl
from jax.experimental.pallas import tpu as pltpu
from jax.sharding import PartitionSpec as P

D = 768
FF = 3072
HD = 64
LAYERS = 2
STEP = 2
SEQ = 4

EPSILON = 1e-05
ROTARY_BASE = 10000.0
BETA_ONE = 0.9
BETA_TWO = 0.999
ADAM_EPSILON = 1e-08
DECAY_RATE = 0.01
SHADOW_RATE = 0.99
CLIP_RATIO = 0.5
RATE_FACTOR = 1.5
SCALES_RATE = 0.6
MASKED = -1000000000.0

HALF = D // 2
TRI = 3 * HALF
HID = FF // 2
BF = jnp.bfloat16
F32 = jnp.float32
MESH = pl.DeviceIdType.MESH
VMEM_BYTES = 60 << 20


def adam_step(weight, moment, square, shadow, gradient, step_rate):
    shadow_decay = min(SHADOW_RATE, (1.0 + STEP) / (10.0 + STEP))
    momentum = BETA_ONE * moment + (1.0 - BETA_ONE) * gradient
    variance = BETA_TWO * square + (1.0 - BETA_TWO) * gradient * gradient
    corrected = (
        momentum
        / (1.0 - BETA_ONE**STEP)
        / (jnp.sqrt(variance / (1.0 - BETA_TWO**STEP)) + ADAM_EPSILON)
    )
    updated = weight - step_rate * (corrected + DECAY_RATE * weight)
    average = shadow_decay * shadow + (1.0 - shadow_decay) * updated
    return (updated, momentum, variance, average)


def nn(a, b):
    return lax.dot_general(a, b, (((1,), (0,)), ((), ())), preferred_element_type=F32)


def nt(a, b):
    return lax.dot_general(a, b, (((1,), (1,)), ((), ())), preferred_element_type=F32)


def tn(a, b):
    return lax.dot_general(a, b, (((0,), (0,)), ((), ())), preferred_element_type=F32)


def place():
    s = lax.axis_index("seq")
    x = lax.div(s, 2)
    c = lax.rem(s, 2)
    return lax.axis_index("dp"), x, c, lax.rem(s + 2, SEQ), s + 1 - 2 * c


def greet(d, peer, sib):
    barrier = pltpu.get_barrier_semaphore()
    for other in (peer, sib):
        pl.semaphore_signal(barrier, inc=1, device_id=(d, other), device_id_type=MESH)
    pl.semaphore_wait(barrier, 2)


def rows_of(c, n):
    return pl.ds(pl.multiple_of(c * n, n), n)


class Copies:
    def __init__(self, lsem, ssem, rsem, d):
        self.lsem, self.ssem, self.rsem, self.d = lsem, ssem, rsem, d
        self.n_local = 0
        self.n_remote = 0

    def local(self, src, dst):
        copy = pltpu.make_async_copy(src, dst, self.lsem.at[self.n_local])
        self.n_local += 1
        copy.start()
        return copy

    def push(self, src, dst, to):
        copy = pltpu.make_async_remote_copy(
            src_ref=src,
            dst_ref=dst,
            send_sem=self.ssem.at[self.n_remote],
            recv_sem=self.rsem.at[self.n_remote],
            device_id=(self.d, to),
            device_id_type=MESH,
        )
        self.n_remote += 1
        copy.start()
        return copy


def norm_stats(values):
    center = values - jnp.mean(values, axis=-1, keepdims=True)
    spread = jnp.mean(center * center, axis=-1, keepdims=True)
    scale = lax.rsqrt(spread + EPSILON)
    return center * scale, scale


def norm_back(values, gain, dy):
    xhat, scale = norm_stats(values)
    u = gain * dy
    du = u - jnp.mean(u, axis=-1, keepdims=True)
    back = scale * (du - xhat * jnp.mean(u * xhat, axis=-1, keepdims=True))
    rows = jnp.concatenate(
        [jnp.sum(xhat * dy, axis=0, keepdims=True), jnp.sum(dy, axis=0, keepdims=True)], axis=0
    )
    return back, rows


def turn(chunk, cosine, sine):
    lane = lax.broadcasted_iota(jnp.int32, chunk.shape, 1)
    swapped = jnp.where(
        lax.rem(lane, HD) < HD // 2, pltpu.roll(chunk, 128 - HD // 2, 1), pltpu.roll(chunk, HD // 2, 1)
    )
    return chunk * cosine + swapped * sine


def half_of(pair, which):
    lane = lax.broadcasted_iota(jnp.int32, pair.shape, 1)
    keep = (lane < HD) if which == 0 else (lane >= HD)
    return jnp.where(keep, pair, jnp.zeros_like(pair))


def attend_fwd_kernel(
    h, wa, sc, cs, bias, mid, na_o, q_o, k_o, v_o, ctx_o, lse_o,
    wt, wo, na, q, k, v, ctxt, ctx, lse, psend, precv, lsem, ssem, rsem,
):
    d, x, c, peer, sib = place()
    y = 1 - x
    rows = h.shape[0]
    copies = Copies(lsem, ssem, rsem, d)
    greet(d, peer, sib)
    wt_own, wo_own = wt.at[rows_of(c, HALF), :], wo.at[:, rows_of(c, HALF)]
    tri_part, out_part = wa.at[:, pl.ds(0, TRI)], wa.at[:, pl.ds(TRI, HALF)]
    tri_sent = copies.push(tri_part, wt_own, sib)
    tri_local = copies.local(tri_part, wt_own)
    out_sent = copies.push(out_part, wo_own, sib)
    out_local = copies.local(out_part, wo_own)
    xhat, _ = norm_stats(h[...])
    na[x] = (xhat * sc[0:1, :] + sc[1:2, :]).astype(BF)
    na_sent = copies.push(na.at[x], na.at[x], peer)
    tri_local.wait()
    tri_sent.wait()

    def project(block):
        cosine, sine = cs[block, :, 0:128], cs[block, :, 128:256]
        for j in range(9):
            part = nn(na[block], wt[:, 128 * j : 128 * j + 128])
            lanes = pl.ds(128 * (j % 3), 128)
            if j < 3:
                q[block, :, lanes] = (turn(part, cosine, sine) * HD**-0.5).astype(BF)
            elif j < 6:
                k[block, rows_of(c, rows), lanes] = turn(part, cosine, sine).astype(BF)
            else:
                v[block, rows_of(c, rows), lanes] = part.astype(BF)

    def share(block):
        mine = (block, rows_of(c, rows))
        return [copies.push(k.at[mine], k.at[mine], sib), copies.push(v.at[mine], v.at[mine], sib)]

    project(x)
    shared = share(x)
    na_sent.wait()
    project(y)
    shared += share(y)
    out_local.wait()
    out_sent.wait()
    for copy in shared:
        copy.wait()

    def attend(block):
        other = 1 - block

        def pair_step(p, carry):
            lanes = pl.ds(pl.multiple_of(p * 128, 128), 128)
            q_pair = q[block, :, lanes]
            k_same, k_cross = k[block, :, lanes], k[other, :, lanes]
            v_same, v_cross = v[block, :, lanes], v[other, :, lanes]
            for which in range(2):
                q_head = half_of(q_pair, which)
                s_same = nt(k_same, q_head)
                s_cross = nt(k_cross, q_head) + bias[0]
                top = jnp.maximum(
                    jnp.max(s_same, axis=0, keepdims=True), jnp.max(s_cross, axis=0, keepdims=True)
                )
                e_same = jnp.exp(s_same - top)
                e_cross = jnp.exp(s_cross - top)
                total = jnp.sum(e_same, axis=0, keepdims=True) + jnp.sum(
                    e_cross, axis=0, keepdims=True
                )
                mixed = tn(v_same, e_same.astype(BF)) + tn(v_cross, e_cross.astype(BF))
                head = pl.ds(pl.multiple_of(p * 128 + which * HD, HD), HD)
                ctxt[head, :] = mixed[which * HD : which * HD + HD, :] / total
                lse[block, pl.ds(2 * p + which, 1), :] = top + jnp.log(total)
            return carry

        lax.fori_loop(0, HALF // 128, pair_step, 0)
        ctx[block] = ctxt[...].T.astype(BF)
        return nn(ctx[block], wo[...])

    psend[...] = attend(y).astype(BF)
    part_sent = copies.push(psend, precv, peer)
    mid[...] = h[...] + attend(x)
    saves = [
        copies.local(a, b)
        for a, b in ((na, na_o), (q, q_o), (k, k_o), (v, v_o), (ctx, ctx_o), (lse, lse_o))
    ]
    part_sent.wait()
    mid[...] = mid[...] + precv[...].astype(F32)
    for copy in saves:
        copy.wait()


def hbm():
    return pl.BlockSpec(memory_space=pl.ANY)


def vmem():
    return pl.BlockSpec(memory_space=pltpu.VMEM)


def call(kernel, name, number, ins, outs, out_shape, scratch, n_local, n_remote, flops, args):
    return pl.pallas_call(
        kernel,
        name=name,
        out_shape=out_shape,
        in_specs=ins,
        out_specs=outs,
        scratch_shapes=[
            *scratch,
            pltpu.SemaphoreType.DMA((n_local,)),
            pltpu.SemaphoreType.DMA((n_remote,)),
            pltpu.SemaphoreType.DMA((n_remote,)),
        ],
        cost_estimate=pl.CostEstimate(flops=flops, bytes_accessed=16 << 20, transcendentals=0),
        compiler_params=pltpu.CompilerParams(
            collective_id=number, has_side_effects=True, vmem_limit_bytes=VMEM_BYTES
        ),
    )(*args)


def sds(shape, dtype):
    return jax.ShapeDtypeStruct(shape, dtype)


def attend_fwd(h, wa, scales, tables, bias):
    t = h.shape[0]
    return call(
        attend_fwd_kernel, "attend_fwd", 0,
        [vmem(), hbm(), vmem(), vmem(), pl.BlockSpec(memory_space=pltpu.SMEM)],
        [vmem()] + [hbm()] * 6,
        [
            sds((t, D), F32), sds((2, t, D), BF), sds((2, t, HALF), BF), sds((2, 2 * t, HALF), BF),
            sds((2, 2 * t, HALF), BF), sds((2, t, HALF), BF), sds((2, 8, t), F32),
        ],
        [
            pltpu.VMEM((D, TRI), BF), pltpu.VMEM((HALF, D), BF), pltpu.VMEM((2, t, D), BF),
            pltpu.VMEM((2, t, HALF), BF), pltpu.VMEM((2, 2 * t, HALF), BF),
            pltpu.VMEM((2, 2 * t, HALF), BF), pltpu.VMEM((HALF, t), F32),
            pltpu.VMEM((2, t, HALF), BF), pltpu.VMEM((2, 8, t), F32),
            pltpu.VMEM((t, D), BF), pltpu.VMEM((t, D), BF),
        ],
        8, 8, 6 << 30, (h, wa, scales, tables, bias),
    )


def gelu_parts(hidden):
    phi_cap = 0.5 * (1.0 + lax.erf(hidden * math.sqrt(0.5)))
    density = jnp.exp(-0.5 * hidden * hidden) * (1.0 / math.sqrt(2.0 * math.pi))
    return hidden * phi_cap, phi_cap + hidden * density


def feed_fwd_kernel(
    mid, wf, sc, h_next, nb_o, act_o, slope_o,
    we, ws, nb, act, slope, psend, precv, lsem, ssem, rsem,
):
    d, x, c, peer, sib = place()
    y = 1 - x
    copies = Copies(lsem, ssem, rsem, d)
    greet(d, peer, sib)
    xhat, _ = norm_stats(mid[...])
    nb[x] = (xhat * sc[2:3, :] + sc[3:4, :]).astype(BF)
    nb_sent = copies.push(nb.at[x], nb.at[x], peer)
    we_own, ws_own = we.at[:, rows_of(c, D)], ws.at[rows_of(c, D), :]
    exp_part, shr_part = wf.at[:, pl.ds(0, D)], wf.at[:, pl.ds(D, D)]
    weights = [
        copies.local(exp_part, we_own),
        copies.push(exp_part, we_own, sib),
        copies.local(shr_part, ws_own),
        copies.push(shr_part, ws_own, sib),
    ]
    for copy in weights:
        copy.wait()

    def feed(block):
        def step(i, carry):
            lanes = pl.ds(pl.multiple_of(i * 256, 256), 256)
            value, rate = gelu_parts(nn(nb[block], we[:, lanes]))
            act[block, :, lanes] = value.astype(BF)
            slope[block, :, lanes] = rate.astype(BF)
            return carry

        lax.fori_loop(0, HID // 256, step, 0)
        return nn(act[block], ws[...])

    h_next[...] = mid[...] + feed(x)
    nb_sent.wait()
    psend[...] = feed(y).astype(BF)
    part_sent = copies.push(psend, precv, peer)
    saves = [copies.local(a, b) for a, b in ((nb, nb_o), (act, act_o), (slope, slope_o))]
    part_sent.wait()
    h_next[...] = h_next[...] + precv[...].astype(F32)
    for copy in saves:
        copy.wait()


def feed_fwd(mid, wf, scales):
    t = mid.shape[0]
    return call(
        feed_fwd_kernel, "feed_fwd", 1,
        [vmem(), hbm(), vmem()],
        [vmem()] + [hbm()] * 3,
        [sds((t, D), F32), sds((2, t, D), BF), sds((2, t, HID), BF), sds((2, t, HID), BF)],
        [
            pltpu.VMEM((D, HID), BF), pltpu.VMEM((HID, D), BF), pltpu.VMEM((2, t, D), BF),
            pltpu.VMEM((2, t, HID), BF), pltpu.VMEM((2, t, HID), BF),
            pltpu.VMEM((t, D), BF), pltpu.VMEM((t, D), BF),
        ],
        5, 4, 5 << 30, (mid, wf, scales),
    )


def feed_bwd_kernel(
    g, mid, wf, sc, nb_h, act_h, slope_h, mid_grad, wg_o, rows_o,
    we, ws, nb, act, slope, gl, hg, part, psend, precv, gown, gsend, grecv, lsem, ssem, rsem,
):
    d, x, c, peer, sib = place()
    y = 1 - x
    t = g.shape[0]
    copies = Copies(lsem, ssem, rsem, d)
    greet(d, peer, sib)
    gl[x] = g[...].astype(BF)
    g_sent = copies.push(gl.at[x], gl.at[x], peer)
    we_own, ws_own = we.at[:, rows_of(c, D)], ws.at[rows_of(c, D), :]
    exp_part, shr_part = wf.at[:, pl.ds(0, D)], wf.at[:, pl.ds(D, D)]
    weights = [
        copies.local(shr_part, ws_own),
        copies.push(shr_part, ws_own, sib),
        copies.local(exp_part, we_own),
        copies.push(exp_part, we_own, sib),
        copies.local(slope_h, slope),
        copies.local(act_h, act),
        copies.local(nb_h, nb),
    ]
    for copy in weights:
        copy.wait()

    def back(block):
        def step(i, carry):
            lanes = pl.ds(pl.multiple_of(i * 256, 256), 256)
            pulled = nt(gl[block], ws[lanes, :])
            hg[block, :, lanes] = (pulled * slope[block, :, lanes].astype(F32)).astype(BF)
            return carry

        lax.fori_loop(0, HID // 256, step, 0)
        return nt(hg[block], we[...])

    part[...] = back(x)
    g_sent.wait()
    psend[...] = back(y).astype(BF)
    part_sent = copies.push(psend, precv, peer)

    gl_all = gl[...].reshape(2 * t, D)
    nb_all = nb[...].reshape(2 * t, D)

    def grads(which, store):
        def step(i, carry):
            at = pl.ds(pl.multiple_of(i * 256, 256), 256)
            off = pl.ds(pl.multiple_of(which * D + i * 256, 256), 256)
            hg_part = hg[:, :, off].reshape(2 * t, 256)
            act_part = act[:, :, off].reshape(2 * t, 256)
            store(0, at, tn(nb_all, hg_part))
            store(1, at, tn(act_part, gl_all))
            return carry

        lax.fori_loop(0, D // 256, step, 0)

    def to_send(kind, at, value):
        if kind == 0:
            gsend[:, at] = value.astype(BF)
        else:
            gsend[at, pl.ds(D, D)] = value.astype(BF)

    def to_keep(kind, at, value):
        if kind == 0:
            gown[:, at] = value
        else:
            gown[at, pl.ds(D, D)] = value

    grads(1 - c, to_send)
    grad_sent = copies.push(gsend, grecv, sib)
    grads(c, to_keep)
    part_sent.wait()
    dy = part[...] + precv[...].astype(F32)
    back_mid, rows = norm_back(mid[...], sc[2:3, :], dy)
    mid_grad[...] = g[...] + back_mid
    rows_o[...] = rows
    grad_sent.wait()
    gsend[...] = (gown[...] + grecv[...].astype(F32)).astype(BF)
    copies.local(gsend, wg_o).wait()


def feed_bwd(g, mid, wf, scales, nb, act, slope):
    t = g.shape[0]
    return call(
        feed_bwd_kernel, "feed_bwd", 2,
        [vmem(), vmem(), hbm(), vmem(), hbm(), hbm(), hbm()],
        [vmem(), hbm(), vmem()],
        [sds((t, D), F32), sds((D, 2 * D), BF), sds((2, D), F32)],
        [
            pltpu.VMEM((D, HID), BF), pltpu.VMEM((HID, D), BF), pltpu.VMEM((2, t, D), BF),
            pltpu.VMEM((2, t, HID), BF), pltpu.VMEM((2, t, HID), BF), pltpu.VMEM((2, t, D), BF),
            pltpu.VMEM((2, t, HID), BF), pltpu.VMEM((t, D), F32), pltpu.VMEM((t, D), BF),
            pltpu.VMEM((t, D), BF), pltpu.VMEM((D, 2 * D), F32), pltpu.VMEM((D, 2 * D), BF),
            pltpu.VMEM((D, 2 * D), BF),
        ],
        6, 5, 10 << 30, (g, mid, wf, scales, nb, act, slope),
    )


def attend_bwd_kernel(
    mg, h, wa, sc, cs, bias, na, q, k, v, ctx, lse, g_prev, wg_o, rows_o,
    wt, wo, ml, cg, delta, dqt, dk, dv, kvsend, kvrecv, pg, part, psend, precv,
    gown, gsend, grecv, lsem, ssem, rsem,
):
    d, x, c, peer, sib = place()
    y = 1 - x
    t = mg.shape[0]
    copies = Copies(lsem, ssem, rsem, d)
    greet(d, peer, sib)
    ml[x] = mg[...].astype(BF)
    ml_sent = copies.push(ml.at[x], ml.at[x], peer)
    wt_own, wo_own = wt.at[rows_of(c, HALF), :], wo.at[:, rows_of(c, HALF)]
    tri_part, out_part = wa.at[:, pl.ds(0, TRI)], wa.at[:, pl.ds(TRI, HALF)]
    out_moves = [copies.local(out_part, wo_own), copies.push(out_part, wo_own, sib)]
    tri_moves = [copies.local(tri_part, wt_own), copies.push(tri_part, wt_own, sib)]
    dk[...] = jnp.zeros_like(dk)
    dv[...] = jnp.zeros_like(dv)
    for copy in out_moves:
        copy.wait()

    def attend(block):
        other = 1 - block
        pulled = nt(ml[block], wo[...])
        cg[block] = pulled.astype(BF)
        weighed = (cg[block].astype(F32) * ctx[block].astype(F32)).T
        for head in range(HALF // HD):
            delta[head : head + 1, :] = jnp.sum(
                weighed[head * HD : head * HD + HD, :], axis=0, keepdims=True
            )

        def pair_step(p, carry):
            lanes = pl.ds(pl.multiple_of(p * 128, 128), 128)
            q_pair, cg_pair = q[block, :, lanes], cg[block, :, lanes]
            for which in range(2):
                q_head, cg_head = half_of(q_pair, which), half_of(cg_pair, which)
                row = pl.ds(2 * p + which, 1)
                total, dots = lse[block, row, :], delta[row, :]
                turned = None
                for side in (block, other):
                    k_pair, v_pair = k[side, :, lanes], v[side, :, lanes]
                    scores = nt(k_pair, q_head)
                    if side is other:
                        scores = scores + bias[0]
                    probs = jnp.exp(scores - total)
                    score_grad = (probs * (nt(v_pair, cg_head) - dots)).astype(BF)
                    dv[side, :, lanes] += nn(probs.astype(BF), cg_head)
                    dk[side, :, lanes] += nn(score_grad, q_head)
                    piece = tn(k_pair, score_grad)
                    turned = piece if turned is None else turned + piece
                head = pl.ds(pl.multiple_of(p * 128 + which * HD, HD), HD)
                dqt[block, head, :] = turned[which * HD : which * HD + HD, :] * HD**-0.5
            return carry

        lax.fori_loop(0, HALF // 128, pair_step, 0)

    attend(x)
    ml_sent.wait()
    attend(y)
    theirs, mine = rows_of(1 - c, t), rows_of(c, t)
    for side in range(2):
        kvsend[side, :, pl.ds(0, HALF)] = dk[side, theirs, :].astype(BF)
        kvsend[side, :, pl.ds(HALF, HALF)] = dv[side, theirs, :].astype(BF)
    kv_sent = copies.push(kvsend, kvrecv, sib)

    def unturn(block, j, value):
        cosine, sine = cs[block, :, 0:128], cs[block, :, 128:256]
        rounded = value.astype(BF).astype(F32)
        pg[block, :, pl.ds(128 * j, 128)] = turn(rounded, cosine, -sine).astype(BF)

    for side in range(2):
        for j in range(3):
            unturn(side, j, dqt[side, 128 * j : 128 * j + 128, :].T)
    kv_sent.wait()
    for side in range(2):
        for j in range(3):
            at = pl.ds(128 * j, 128)
            unturn(side, 3 + j, dk[side, mine, at] + kvrecv[side, :, at].astype(F32))
            pg[side, :, pl.ds(D + 128 * j, 128)] = (
                dv[side, mine, at] + kvrecv[side, :, pl.ds(HALF + 128 * j, 128)].astype(F32)
            ).astype(BF)
    for copy in tri_moves:
        copy.wait()
    psend[...] = nt(pg[y], wt[...]).astype(BF)
    part_sent = copies.push(psend, precv, peer)
    part[...] = nt(pg[x], wt[...])

    ml_all = ml[...].reshape(2 * t, D)
    na_all = na[...].reshape(2 * t, D)
    ctx_all = ctx[...].reshape(2 * t, HALF)

    def grads(which, store):
        def step(i, carry):
            off = pl.ds(pl.multiple_of(which * HALF + i * 128, 128), 128)
            at = pl.ds(pl.multiple_of(i * 128, 128), 128)
            store(0, at, tn(na[:, :, off].reshape(2 * t, 128), pg[...].reshape(2 * t, TRI)))
            store(1, at, tn(ctx_all, ml[:, :, off].reshape(2 * t, 128)))
            return carry

        lax.fori_loop(0, HALF // 128, step, 0)

    def to_send(kind, at, value):
        if kind == 0:
            gsend[at, pl.ds(0, TRI)] = value.astype(BF)
        else:
            gsend[:, pl.ds(pl.multiple_of(TRI + at.start, 128), 128)] = value.astype(BF)

    def to_keep(kind, at, value):
        if kind == 0:
            gown[at, pl.ds(0, TRI)] = value
        else:
            gown[:, pl.ds(pl.multiple_of(TRI + at.start, 128), 128)] = value

    grads(1 - c, to_send)
    grad_sent = copies.push(gsend, grecv, sib)
    grads(c, to_keep)
    part_sent.wait()
    dy = part[...] + precv[...].astype(F32)
    back, rows = norm_back(h[...], sc[0:1, :], dy)
    g_prev[...] = mg[...] + back
    rows_o[...] = rows
    grad_sent.wait()
    gsend[...] = (gown[...] + grecv[...].astype(F32)).astype(BF)
    copies.local(gsend, wg_o).wait()


def attend_bwd(mg, h, wa, scales, tables, bias, saved):
    t = mg.shape[0]
    return call(
        attend_bwd_kernel, "attend_bwd", 3,
        [vmem(), vmem(), hbm(), vmem(), vmem(), pl.BlockSpec(memory_space=pltpu.SMEM)] + [vmem()] * 6,
        [vmem(), hbm(), vmem()],
        [sds((t, D), F32), sds((HALF, 2 * D), BF), sds((2, D), F32)],
        [
            pltpu.VMEM((D, TRI), BF), pltpu.VMEM((HALF, D), BF), pltpu.VMEM((2, t, D), BF),
            pltpu.VMEM((2, t, HALF), BF), pltpu.VMEM((8, t), F32), pltpu.VMEM((2, HALF, t), F32),
            pltpu.VMEM((2, 2 * t, HALF), F32), pltpu.VMEM((2, 2 * t, HALF), F32),
            pltpu.VMEM((2, t, D), BF), pltpu.VMEM((2, t, D), BF), pltpu.VMEM((2, t, TRI), BF),
            pltpu.VMEM((t, D), F32), pltpu.VMEM((t, D), BF), pltpu.VMEM((t, D), BF),
            pltpu.VMEM((HALF, 2 * D), F32), pltpu.VMEM((HALF, 2 * D), BF),
            pltpu.VMEM((HALF, 2 * D), BF),
        ],
        3, 6, 10 << 30, (mg, h, wa, scales, tables, bias, *saved),
    )


class Moves:
    def __init__(self, dp):
        self.dp = dp
        self.d = lax.axis_index("dp")
        s = lax.axis_index("seq")
        self.s, self.x, self.c = s, s // 2, s % 2
        half = dp // 2
        ids = [(d, s) for d in range(dp) for s in range(SEQ)]
        self.tri = []
        for r in range(2):
            for j in range(3):
                perm = []
                for d, s in ids:
                    b = (3 * s + j) % 4
                    to = (2 * (d % half) + (r ^ (b % 2)), 2 * (b // 2) + d // half)
                    perm.append((d * SEQ + s, to[0] * SEQ + to[1]))
                self.tri.append(perm)
        self.out = []
        for r in range(2):
            perm = []
            for d, s in ids:
                to = (2 * (d % half) + (r ^ (s % 2)), 2 * (d // half) + s // 2)
                perm.append((d * SEQ + s, to[0] * SEQ + to[1]))
            self.out.append(perm)
        self.shr = []
        for k in range(4):
            perm = []
            for d, s in ids:
                to = (4 * (d % (dp // 4)) + (k + s) % 4, d // (dp // 4))
                perm.append((d * SEQ + s, to[0] * SEQ + to[1]))
            self.shr.append(perm)

    def send(self, piece, perm, back):
        if back:
            perm = [(b, a) for a, b in perm]
        return lax.ppermute(piece, ("dp", "seq"), perm)

    @staticmethod
    def pick(pieces, index):
        return lax.dynamic_index_in_dim(jnp.stack(pieces), index, 0, keepdims=False)

    def tri_out(self, low):
        n, rows, _ = low.shape
        halves = low.reshape(n, 2, rows // 2, 3, 192)
        got = []
        for r in range(2):
            for j in range(3):
                which = r ^ (((3 * self.s + j) % 4) % 2)
                piece = lax.dynamic_index_in_dim(halves[:, :, :, j], which, 1, keepdims=False)
                got.append(self.send(piece, self.tri[3 * r + j], False))
        parts = []
        for t in range(3):
            for bb in range(2):
                r, j = bb ^ (self.d % 2), (t + 2 * self.x + bb) % 3
                parts.append(self.pick(got, 3 * r + j))
        return jnp.concatenate(parts, axis=-1)

    def tri_back(self, grad):
        n, rows, _ = grad.shape
        got = []
        for r in range(2):
            for j in range(3):
                bb = (self.d % 2) ^ r
                t = (j - (2 * self.x + bb)) % 3
                piece = lax.dynamic_slice_in_dim(grad, (2 * t + bb) * 192, 192, 2)
                got.append(self.send(piece, self.tri[3 * r + j], True))
        cols = []
        for j in range(3):
            two = []
            for hh in range(2):
                r = hh ^ (((3 * self.s + j) % 4) % 2)
                two.append(self.pick([got[j], got[3 + j]], r))
            cols.append(jnp.concatenate(two, axis=1))
        return jnp.concatenate(cols, axis=-1)

    def out_out(self, low):
        n, rows, _ = low.shape
        halves = low.reshape(n, 2, rows // 2, 192)
        got = [
            self.send(
                lax.dynamic_index_in_dim(halves, r ^ (self.s % 2), 1, keepdims=False), self.out[r], False
            )
            for r in range(2)
        ]
        return jnp.concatenate([self.pick(got, u ^ (self.d % 2)) for u in range(2)], axis=-1)

    def out_back(self, grad):
        got = []
        for r in range(2):
            u = r ^ (self.d % 2)
            got.append(self.send(lax.dynamic_slice_in_dim(grad, u * 192, 192, 2), self.out[r], True))
        return jnp.concatenate([self.pick(got, hh ^ (self.s % 2)) for hh in range(2)], axis=1)

    def shr_out(self, low):
        n, rows, _ = low.shape
        subs = low.reshape(n, 4, rows // 4, 192)
        got = [
            self.send(
                lax.dynamic_index_in_dim(subs, (k + self.s) % 4, 1, keepdims=False), self.shr[k], False
            )
            for k in range(4)
        ]
        return jnp.concatenate([self.pick(got, (self.d - s) % 4) for s in range(4)], axis=-1)

    def shr_back(self, grad):
        got = []
        for k in range(4):
            piece = lax.dynamic_slice_in_dim(grad, ((self.d - k) % 4) * 192, 192, 2)
            got.append(self.send(piece, self.shr[k], True))
        return jnp.concatenate([self.pick(got, (sub - self.s) % 4) for sub in range(4)], axis=1)


def tables_here(segments, t, x, c):
    group = segments.shape[0]
    whole = segments[0] == segments[group - 1]
    place_in_half = c * t + jnp.arange(t, dtype=jnp.int32)
    second = jnp.where(whole, group // 2, 0).astype(jnp.int32)
    positions = jnp.stack([place_in_half, place_in_half + second]).astype(F32)
    lane = jnp.arange(128, dtype=jnp.int32)
    inverse = 1.0 / ROTARY_BASE ** ((lane % (HD // 2)).astype(F32) * (2.0 / HD))
    angles = positions[:, :, None] * inverse[None, None, :]
    sign = jnp.where(lane % HD < HD // 2, -1.0, 1.0).astype(F32)
    tables = jnp.concatenate([jnp.cos(angles), jnp.sin(angles) * sign], axis=-1)
    bias = jnp.where(whole, 0.0, MASKED).astype(F32).reshape(1)
    return tables, bias


def local(dp, *args):
    (residual, cotangent, segments) = args[:3]
    (
        triple_weight, triple_moment, triple_square, triple_shadow,
        output_weight, output_moment, output_square, output_shadow,
        expand_weight, expand_moment, expand_square, expand_shadow,
        shrink_weight, shrink_moment, shrink_square, shrink_shadow,
        scales_weight, scales_moment, scales_square, scales_shadow,
    ) = args[3:]
    moves = Moves(dp)
    t = residual.shape[0]
    d, s = lax.axis_index("dp"), lax.axis_index("seq")
    tables, bias = tables_here(segments, t, moves.x, moves.c)

    scales_all = lax.psum(
        lax.dynamic_update_slice(
            jnp.zeros((LAYERS, 4, D), F32), scales_weight.astype(BF).astype(F32), (0, s, d * (D // dp))
        ),
        ("dp", "seq"),
    )
    tri = moves.tri_out(triple_weight.astype(BF))
    out = moves.out_out(output_weight.astype(BF))
    shr = moves.shr_out(shrink_weight.astype(BF))
    attend_parts = jnp.concatenate([tri, out], axis=-1)
    feed_parts = jnp.concatenate([expand_weight.astype(BF), shr], axis=-1)
    gather = functools.partial(lax.all_gather, axis_name="dp", axis=0, tiled=True)
    wa, wf = [], []
    for layer in range(LAYERS):
        wa.append(gather(attend_parts[layer]))
        wf.append(gather(feed_parts[layer]))

    stream = residual
    kept = []
    for layer in range(LAYERS):
        scales = scales_all[layer]
        middle, *attend_saved = attend_fwd(stream, wa[layer], scales, tables, bias)
        following, *feed_saved = feed_fwd(middle, wf[layer], scales)
        kept.append((stream, middle, attend_saved, feed_saved))
        stream = following

    g = cotangent
    attend_grads, feed_grads, scale_grads = [None] * LAYERS, [None] * LAYERS, [None] * LAYERS
    scatter = functools.partial(lax.psum_scatter, axis_name="dp", scatter_dimension=0, tiled=True)
    for layer in reversed(range(LAYERS)):
        scales = scales_all[layer]
        h, middle, attend_saved, feed_saved = kept[layer]
        mg, feed_grad, rows_b = feed_bwd(g, middle, wf[layer], scales, *feed_saved)
        feed_grads[layer] = scatter(feed_grad).astype(F32)
        g, attend_grad, rows_a = attend_bwd(mg, h, wa[layer], scales, tables, bias, attend_saved)
        attend_grads[layer] = scatter(attend_grad).astype(F32)
        scale_grads[layer] = jnp.concatenate([rows_a, rows_b], axis=0)

    scale_grad = lax.psum(jnp.stack(scale_grads), ("dp", "seq"))
    own_scale = lax.dynamic_slice(scale_grad, (0, s, d * (D // dp)), (LAYERS, 1, D // dp))
    squares = jnp.sum(own_scale * own_scale)
    for part in (*attend_grads, *feed_grads):
        squares = squares + jnp.sum(part * part)
    grad_norm = jnp.sqrt(lax.psum(squares, ("dp", "seq")))
    limit = CLIP_RATIO * math.sqrt(float(LAYERS * (4 * D * D + 2 * D * FF + 4 * D)))
    factor = limit / (grad_norm + 1e-06)

    attend_grad, feed_grad = jnp.stack(attend_grads).astype(BF), jnp.stack(feed_grads).astype(BF)
    triple_grad = moves.tri_back(attend_grad[:, :, :TRI]).astype(F32)
    output_grad = moves.out_back(attend_grad[:, :, TRI:]).astype(F32)
    expand_grad = feed_grad[:, :, :D].astype(F32)
    shrink_grad = moves.shr_back(feed_grad[:, :, D:]).astype(F32)

    results = [stream, g, grad_norm]
    for weight, moment, square, shadow, grad, rate in (
        (triple_weight, triple_moment, triple_square, triple_shadow, triple_grad, RATE_FACTOR / math.sqrt(D)),
        (output_weight, output_moment, output_square, output_shadow, output_grad, RATE_FACTOR / math.sqrt(D // 16)),
        (expand_weight, expand_moment, expand_square, expand_shadow, expand_grad, RATE_FACTOR / math.sqrt(D)),
        (shrink_weight, shrink_moment, shrink_square, shrink_shadow, shrink_grad, RATE_FACTOR / math.sqrt(FF)),
        (scales_weight, scales_moment, scales_square, scales_shadow, own_scale, SCALES_RATE),
    ):
        results.extend(adam_step(weight, moment, square, shadow, grad * factor, rate))
    return tuple(results)


def solution(mesh):
    token = P(("dp", "seq"), None)
    weight = P(None, "dp", "seq")
    scale = P(None, "seq", "dp")
    return jax.shard_map(
        functools.partial(local, mesh.shape["dp"]),
        mesh=mesh,
        in_specs=(token, token, P("dp"), *([weight] * 16), *([scale] * 4)),
        out_specs=(token, token, P(), *([weight] * 16), *([scale] * 4)),
        check_vma=False,
    )
```

time: 2110 us -> 754 us (0.36)
  waiting for transfers between devices: 1450 us -> 249 us
  Pallas kernels: 0 us -> 242 us
  matrix products: 173 us -> 0 us
  local copies, waits for them, and re-layouts: 119 us -> 10.9 us
  blocking collectives: 199 us -> 133 us
  other arithmetic: 73.3 us -> 25.9 us
    reduce_scatter x10 -> x4, waiting for transfers between devices: 932 us -> 209 us  [the longest x2 123 us: local(): feed_grads[layer] = scatter(feed_grad).astype(F32)]
    pallas_call x0 -> x8, Pallas kernels: none -> 242 us  [call(): pl.pallas_call(kernel, name=name, out_shape=out_shape, in_specs=ins, out_...]
    unnamed x34 -> x8, waiting for transfers between devices: 240 us -> 3.17 us
    dot_general x52 -> x0, matrix products: 173 us -> none  [the longest x8 38.4 us: over_rows(): lax.dot_general(left_side, right_side, (((0,), (0,)), ((), ())), preferre...]
    all_gather x8 -> x4, waiting for transfers between devices: 203 us -> 31.2 us  [the longest x2 22.4 us: local(): wf.append(gather(feed_parts[layer]))]
    all_gather x12 -> x0, blocking collectives: 154 us -> none  [the longest x2 64.8 us: local(): lax.all_gather(lax.all_gather(scales_weight[layer_index].astype(jnp.bfloa...]
    psum x1 -> x3, blocking collectives: 39.4 us -> 133 us  [the longest x1 53.8 us: local(): lax.psum(lax.dynamic_update_slice(jnp.zeros((LAYERS, 4, D), F32), scales_...]
    all_to_all x16 -> x0, waiting for transfers between devices: 77.6 us -> none  [the longest x2 14.7 us: backward_layer(): lax.all_to_all(context_grad, 'seq', split_axis=1, concat_axis=0, tiled=True)]
  transfers between devices with their start and end apart: 42 -> 32, of which waited for: 33 -> 9; matrix products, arithmetic and copies ran while one was open for 14% -> 3% of each run, Pallas kernels for 0% -> 12%
where the time goes in v1:
time: 754 us; the launch traced here: 744 us
  waiting for transfers between devices  249 us (33%)
  Pallas kernels  242 us (32%)
  blocking collectives  133 us (18%)
  starting transfers between devices  60.9 us (8%)
  other arithmetic  25.9 us (3%)
  between operations  22.8 us (3%)
  local copies, waits for them, and re-layouts  10.9 us (1%)
    pallas_call x8, Pallas kernels, call(): pl.pallas_call(kernel, name=name, out_shape=out_shape, in_specs=ins, out_...  242 us
    reduce_scatter x2, waiting for transfers between devices, local(): feed_grads[layer] = scatter(feed_grad).astype(F32)  123 us
    reduce_scatter x2, waiting for transfers between devices, local(): attend_grads[layer] = scatter(attend_grad).astype(F32)  86.6 us
    ppermute x24, starting transfers between devices, send(): return lax.ppermute(piece, ('dp', 'seq'), perm)  60.6 us
    psum x1, blocking collectives, local(): lax.psum(lax.dynamic_update_slice(jnp.zeros((LAYERS, 4, D), F32), scales_...  53.8 us
    psum x1, blocking collectives, local(): scale_grad = lax.psum(jnp.stack(scale_grads), ('dp', 'seq'))  39.8 us
    psum x1, blocking collectives, local(): grad_norm = jnp.sqrt(lax.psum(squares, ('dp', 'seq')))  39.5 us
    all_gather x2, waiting for transfers between devices, local(): wf.append(gather(feed_parts[layer]))  22.4 us
  transfers between devices with their start and end apart: 32, of which 9 were waited for; matrix products, arithmetic and copies ran while one was open for 3% of the time, Pallas kernels for 12%

profile of v1, /device:TPU:0, one launch (start us, length us, event | category | flops | bytes accessed | tf_op | source)
XLA Modules:
  0.0 744.4 jit_solution(9064784373259453144)
XLA Ops:
  10.5 5.8 collective-permute-start.1
  16.3 3.4 collective-permute-start.2
  22.7 4.9 collective-permute-start.5
  28.3 3.1 collective-permute-start.7
  35.8 5.6 collective-permute-start.11
  41.7 5.2 collective-permute-start.9
  47.8 2.7 collective-permute-done.10
  56.8 53.8 %psum.21 = f32[2,4,768]{2,1,0:T(4,128)S(1)} all-reduce(f32[2,4,768]{2,1,0:T(4,128)S(1)} %dynamic_update_slice.3), channel_id=1, replica_groups=mesh['dp'=8,'seq'=4] {'dp','seq'}, use_global_device_ids=true, to_apply=%region_0.1 | all-reduce | flops 6144 | bytes 49152 | tf_op jit(solution)/shard_map/psum | solution.py:735
  113.1 31.5 %attend_fwd.2 = (f32[256,768]{1,0:T(8,128)}, bf16[2,256,768]{2,1,0:T(8,128)(2,1)}, bf16[2,256,384]{2,1,0:T(8,128)(2,1)}, bf16[2,512,384]{2,1,0:T(8,128)(2,1)}, b...) custom-call(f32[256,768]{1,0:T(8,128)} %h.3, bf16[384,1536]{1,0:T(8,128)(2,1)} %bitcast.159, ...), custom_call_target="tpu_custom_call" | custom-call | flops 6442450944 | bytes 16777216 | tf_op jit(solution)/shard_map/attend_fwd/pallas_call | solution.py:240
  144.6 26.1 %feed_fwd.2 = (f32[256,768]{1,0:T(8,128)}, bf16[2,256,768]{2,1,0:T(8,128)(2,1)}, bf16[2,256,1536]{2,1,0:T(8,128)(2,1)}, bf16[2,256,1536]{2,1,0:T(8,128)(2,1)}) custom-call(f32[256,768]{1,0:T(8,128)} %get-tuple-element.57.mid, bf16[768,1536]{1,0:T(8,128)(2,1)} %bitcast.155, f32[4,768]{1,0:T(4,128)} %get-tuple-element.190.sc), custom_call_target="tpu_custom_call" | custom-call | flops 5368709120 | bytes 16777216 | tf_op jit(solution)/shard_map/feed_fwd/pallas_call | solution.py:240
  170.7 8.9 %all-gather.13.cloned.1.call-done = bf16[1,384,1536]{2,1,0:T(8,128)(2,1)} async-done(((bf16[1,48,1536]{2,1,0:T(8,128)(2,1)}), bf16[1,384,1536]{2,1,0:T(8,128)(2,1)}) %all-gather.13.cloned.1.call-update) | async-done | bytes 1179664 | tf_op jit(solution)/shard_map/all_gather | solution.py:749
  179.5 31.1 %attend_fwd.3 = (f32[256,768]{1,0:T(8,128)}, bf16[2,256,768]{2,1,0:T(8,128)(2,1)}, bf16[2,256,384]{2,1,0:T(8,128)(2,1)}, bf16[2,512,384]{2,1,0:T(8,128)(2,1)}, b...) custom-call(f32[256,768]{1,0:T(8,128)} %get-tuple-element.58.h, ...), custom_call_target="tpu_custom_call" | custom-call | flops 6442450944 | bytes 16777216 | tf_op jit(solution)/shard_map/attend_fwd/pallas_call | solution.py:240
  210.7 22.3 %all-gather.15.cloned.1.call-done = bf16[1,768,1536]{2,1,0:T(8,128)(2,1)} async-done(((bf16[1,96,1536]{2,1,0:T(8,128)(2,1)}), bf16[1,768,1536]{2,1,0:T(8,128)(2,1)}) %all-gather.15.cloned.1.call-update) | async-done | bytes 2359312 | tf_op jit(solution)/shard_map/all_gather | solution.py:750
  233.0 24.8 %feed_fwd.3 = (f32[256,768]{1,0:T(8,128)}, bf16[2,256,768]{2,1,0:T(8,128)(2,1)}, bf16[2,256,1536]{2,1,0:T(8,128)(2,1)}, bf16[2,256,1536]{2,1,0:T(8,128)(2,1)}) custom-call(f32[256,768]{1,0:T(8,128)} %get-tuple-element.59.mid, bf16[768,1536]{1,0:T(8,128)(2,1)} %bitcast.157, f32[4,768]{1,0:T(4,128)} %get-tuple-element.189.sc), custom_call_target="tpu_custom_call" | custom-call | flops 5368709120 | bytes 16777216 | tf_op jit(solution)/shard_map/feed_fwd/pallas_call | solution.py:240
  257.8 28.5 %feed_bwd.2 = (f32[256,768]{1,0:T(8,128)}, bf16[768,1536]{1,0:T(8,128)(2,1)}, f32[2,768]{1,0:T(2,128)}) custom-call(f32[256,768]{1,0:T(8,128)} %g.1, f32[256,768]{1,0:T(8,128)} %get-tuple-element.59.mid, bf16[768,1536]{1,0:T(8,128)(2,1)} %bitcast.158, f32[4,768]{1,0:T(4,128)} %get-tuple-element.189.sc, bf16[2,256,768]{2,1,0:T(8,128)(2,1)} %get-tuple-element.61.nb_h, ...), custom_call_target="tpu_custom_call" | custom-call | flops 10737418240 | bytes 16777216 | tf_op jit(solution)/shard_map/feed_bwd/pallas_call | solution.py:240
  286.3 36.5 %attend_bwd.2 = (f32[256,768]{1,0:T(8,128)}, bf16[384,1536]{1,0:T(8,128)(2,1)}, f32[2,768]{1,0:T(2,128)}) custom-call(f32[256,768]{1,0:T(8,128)} %get-tuple-element.64.mg, f32[256,768]{1,0:T(8,128)} %get-tuple-element.58.h, bf16[384,1536]{1,0:T(8,128)(2,1)} %bitcast.162, f32[4,768]{1,0:T(4,128)} %get-tuple-element.189.sc, ...), custom_call_target="tpu_custom_call" | custom-call | flops 10737418240 | bytes 16777216 | tf_op jit(solution)/shard_map/attend_bwd/pallas_call | solution.py:240
  322.9 27.8 %feed_bwd.3 = (f32[256,768]{1,0:T(8,128)}, bf16[768,1536]{1,0:T(8,128)(2,1)}, f32[2,768]{1,0:T(2,128)}) custom-call(f32[256,768]{1,0:T(8,128)} %get-tuple-element.71.g, f32[256,768]{1,0:T(8,128)} %get-tuple-element.57.mid, bf16[768,1536]{1,0:T(8,128)(2,1)} %bitcast.156, f32[4,768]{1,0:T(4,128)} %get-tuple-element.190.sc, ...), custom_call_target="tpu_custom_call" | custom-call | flops 10737418240 | bytes 16777216 | tf_op jit(solution)/shard_map/feed_bwd/pallas_call | solution.py:240
  350.7 35.6 %attend_bwd.3 = (f32[256,768]{1,0:T(8,128)}, bf16[384,1536]{1,0:T(8,128)(2,1)}, f32[2,768]{1,0:T(2,128)}) custom-call(f32[256,768]{1,0:T(8,128)} %get-tuple-element.75.mg, f32[256,768]{1,0:T(8,128)} %h.3, bf16[384,1536]{1,0:T(8,128)(2,1)} %bitcast.160, f32[4,768]{1,0:T(4,128)} %get-tuple-element.190.sc, f32[2,256,256]{2,1,0:T(8,128)} %pad_maximum_fusion.cs, ...), custom_call_target="tpu_custom_call" | custom-call | flops 10737418240 | bytes 16777216 | tf_op jit(solution)/shard_map/attend_bwd/pallas_call | solution.py:240
  388.8 39.8 %psum.22 = f32[2,4,768]{2,1,0:T(4,128)S(1)} all-reduce(f32[2,4,768]{2,1,0:T(4,128)S(1)} %pad_maximum_fusion.5), channel_id=1, replica_groups=mesh['dp'=8,'seq'=4] {'dp','seq'}, use_global_device_ids=true, to_apply=%region_1.2 | all-reduce | flops 6144 | bytes 49152 | tf_op jit(solution)/shard_map/psum | solution.py:773
  429.3 20.3 %reduce-scatter.5.cloned.1.call-done = bf16[48,1536]{1,0:T(8,128)(2,1)} async-done(((bf16[384,1536]{1,0:T(8,128)(2,1)}), bf16[48,1536]{1,0:T(8,128)(2,1)}) %reduce-scatter.5.cloned.1.call-update) | async-done | bytes 147472 | tf_op jit(solution)/shard_map/reduce_scatter | solution.py:770
  449.6 66.3 %reduce-scatter.7.cloned.1.call-done = bf16[48,1536]{1,0:T(8,128)(2,1)} async-done(((bf16[384,1536]{1,0:T(8,128)(2,1)}), bf16[48,1536]{1,0:T(8,128)(2,1)}) %reduce-scatter.7.cloned.1.call-update) | async-done | bytes 147472 | tf_op jit(solution)/shard_map/reduce_scatter | solution.py:770
  517.1 3.5 collective-permute-start.16
  530.1 8.0 %collective-permute-start.13 = (bf16[2,48,192]{2,1,0:T(8,128)(2,1)S(1)}, bf16[2,48,192]{2,1,0:T(8,128)(2,1)S(1)}, u32[]{:S(2)}, u32[]{:S(2)}) collective-permute-start(bf16[2,48,192]{2,1,0:T(8,128)(2,1)S(1)} %get-tuple-element.165), channel_id=1, source_target_pairs={{4,0},{2,1},{6,2},{0,3},{12,4},{10,5},{14,6},{8,7},{20,8},{18,9},{... | collective-permute-start | bytes 110600 | tf_op jit(solution)/shard_map/ppermute | solution.py:629
  541.0 52.5 %reduce-scatter.9.cloned.1.call-done = bf16[96,1536]{1,0:T(8,128)(2,1)} async-done(((bf16[768,1536]{1,0:T(8,128)(2,1)}), bf16[96,1536]{1,0:T(8,128)(2,1)}) %reduce-scatter.9.cloned.1.call-update) | async-done | bytes 294928 | tf_op jit(solution)/shard_map/reduce_scatter | solution.py:768
  595.3 70.1 %reduce-scatter.11.cloned.1.call-done = bf16[96,1536]{1,0:T(8,128)(2,1)} async-done(((bf16[768,1536]{1,0:T(8,128)(2,1)}), bf16[96,1536]{1,0:T(8,128)(2,1)}) %reduce-scatter.11.cloned.1.call-update) | async-done | bytes 294928 | tf_op jit(solution)/shard_map/reduce_scatter | solution.py:768
  669.3 39.5 %psum.23 = f32[]{:T(128)} all-reduce(f32[]{:T(128)S(6)} %add.605), channel_id=1, replica_groups=mesh['dp'=8,'seq'=4] {'dp','seq'}, use_global_device_ids=true, to_apply=%region_11.12 | all-reduce | flops 1 | bytes 8 | tf_op jit(solution)/shard_map/psum | solution.py:778
  709.5 2.0 fusion.8
  713.5 2.3 collective-permute-start.22
  715.8 3.7 collective-permute-start.21
  719.5 2.4 collective-permute-start.20
  722.0 2.9 multiply_add_fusion.2
  731.5 2.1 multiply_add_fusion
  (181 shorter events, 48.6 us)
Async XLA Ops:
  7.2 105.9 %all-gather.9.cloned.1.call-start = ((), (), s32[]{:S(2)}) async-start(), calls=%async_computation.8 | async-start | bytes 1327104 | tf_op jit(solution)/shard_map/all_gather | solution.py:749
  9.3 13.4 %collective-permute-start = (bf16[2,48,192]{2,1,0:T(8,128)(2,1)S(1)}, bf16[2,48,192]{2,1,0:T(8,128)(2,1)S(1)}, u32[]{:S(2)}, u32[]{:S(2)}) collective-permute-start(bf16[2,48,192]{2,1,0:T(8,128)(2,1)S(1)} %bitcast.141), channel_id=1, source_target_pairs={{0,0},{1,6},{2,2},{3,4},{4,8},{5,14},{6,10},{7,12},{8,16},{9,22},{... | collective-permute-start | bytes 110600 | tf_op jit(solution)/shard_map/ppermute | solution.py:629
  10.5 17.1 %collective-permute-start.1 = (bf16[2,48,192]{2,1,0:T(8,128)(2,1)S(1)}, bf16[2,48,192]{2,1,0:T(8,128)(2,1)S(1)}, u32[]{:S(2)}, u32[]{:S(2)}) collective-permute-start(bf16[2,48,192]{2,1,0:T(8,128)(2,1)S(1)} %bitcast.145), channel_id=1, source_target_pairs={{0,4},{1,0},{2,6},{3,2},{4,12},{5,8},{6,14},{7,10},{8,20},{9,16},{... | collective-permute-start | bytes 110600 | tf_op jit(solution)/shard_map/ppermute | solution.py:629
  16.3 12.0 %collective-permute-start.2 = (bf16[2,48,192]{2,1,0:T(8,128)(2,1)S(1)}, bf16[2,48,192]{2,1,0:T(8,128)(2,1)S(1)}, u32[]{:S(2)}, u32[]{:S(2)}) collective-permute-start(bf16[2,48,192]{2,1,0:T(8,128)(2,1)S(1)} %bitcast.144), channel_id=1, source_target_pairs={{0,2},{1,4},{2,0},{3,6},{4,10},{5,12},{6,8},{7,14},{8,18},{9,20},{... | collective-permute-start | bytes 110600 | tf_op jit(solution)/shard_map/ppermute | solution.py:629
  19.7 11.7 %collective-permute-start.3 = (bf16[2,48,192]{2,1,0:T(8,128)(2,1)S(1)}, bf16[2,48,192]{2,1,0:T(8,128)(2,1)S(1)}, u32[]{:S(2)}, u32[]{:S(2)}) collective-permute-start(bf16[2,48,192]{2,1,0:T(8,128)(2,1)S(1)} %bitcast.143), channel_id=1, source_target_pairs={{0,4},{1,2},{2,6},{3,0},{4,12},{5,10},{6,14},{7,8},{8,20},{9,18},{... | collective-permute-start | bytes 110600 | tf_op jit(solution)/shard_map/ppermute | solution.py:629
  21.7 9.7 %collective-permute-start.4 = (bf16[2,48,192]{2,1,0:T(8,128)(2,1)S(1)}, bf16[2,48,192]{2,1,0:T(8,128)(2,1)S(1)}, u32[]{:S(2)}, u32[]{:S(2)}) collective-permute-start(bf16[2,48,192]{2,1,0:T(8,128)(2,1)S(1)} %bitcast.142), channel_id=1, source_target_pairs={{0,0},{1,4},{2,2},{3,6},{4,8},{5,12},{6,10},{7,14},{8,16},{9,20},{... | collective-permute-start | bytes 110600 | tf_op jit(solution)/shard_map/ppermute | solution.py:629
  22.7 10.7 %collective-permute-start.5 = (bf16[2,48,192]{2,1,0:T(8,128)(2,1)S(1)}, bf16[2,48,192]{2,1,0:T(8,128)(2,1)S(1)}, u32[]{:S(2)}, u32[]{:S(2)}) collective-permute-start(bf16[2,48,192]{2,1,0:T(8,128)(2,1)S(1)} %bitcast.146), channel_id=1, source_target_pairs={{0,6},{1,0},{2,4},{3,2},{4,14},{5,8},{6,12},{7,10},{8,22},{9,16},{... | collective-permute-start | bytes 110600 | tf_op jit(solution)/shard_map/ppermute | solution.py:629
  27.6 3.9 collective-permute-start.6
  28.3 5.1 collective-permute-start.7
  34.4 110.2 %all-gather.11.cloned.1.call-start = ((), (), s32[]{:S(2)}) async-start(), calls=%async_computation.9 | async-start | bytes 2654208 | tf_op jit(solution)/shard_map/all_gather | solution.py:750
  35.8 12.0 %collective-permute-start.11 = (bf16[2,96,192]{2,1,0:T(8,128)(2,1)S(1)}, bf16[2,96,192]{2,1,0:T(8,128)(2,1)S(1)}, u32[]{:S(2)}, u32[]{:S(2)}) collective-permute-start(bf16[2,96,192]{2,1,0:T(8,128)(2,1)S(1)} %bitcast.137), channel_id=1, source_target_pairs={{0,12},{1,0},{2,4},{3,8},{4,28},{5,16},{6,20},{7,24},{8,13},{9,1},... | collective-permute-start | bytes 221192 | tf_op jit(solution)/shard_map/ppermute | solution.py:629
  41.5 9.0 %collective-permute-start.10 = (bf16[2,96,192]{2,1,0:T(8,128)(2,1)S(1)}, bf16[2,96,192]{2,1,0:T(8,128)(2,1)S(1)}, u32[]{:S(2)}, u32[]{:S(2)}) collective-permute-start(bf16[2,96,192]{2,1,0:T(8,128)(2,1)S(1)} %bitcast.138), channel_id=1, source_target_pairs={{0,8},{1,12},{2,0},{3,4},{4,24},{5,28},{6,16},{7,20},{8,9},{9,13},... | collective-permute-start | bytes 221192 | tf_op jit(solution)/shard_map/ppermute | solution.py:629
  41.7 9.5 %collective-permute-start.9 = (bf16[2,96,192]{2,1,0:T(8,128)(2,1)S(1)}, bf16[2,96,192]{2,1,0:T(8,128)(2,1)S(1)}, u32[]{:S(2)}, u32[]{:S(2)}) collective-permute-start(bf16[2,96,192]{2,1,0:T(8,128)(2,1)S(1)} %bitcast.139), channel_id=1, source_target_pairs={{0,4},{1,8},{2,12},{3,0},{4,20},{5,24},{6,28},{7,16},{8,5},{9,9},{... | collective-permute-start | bytes 221192 | tf_op jit(solution)/shard_map/ppermute | solution.py:629
  47.0 4.2 collective-permute-start.8
  52.6 127.0 %all-gather.13.cloned.1.call-start = ((), (), s32[]{:S(2)}) async-start(), calls=%async_computation.10 | async-start | bytes 1327104 | tf_op jit(solution)/shard_map/all_gather | solution.py:749
  53.3 179.7 %all-gather.15.cloned.1.call-start = ((), (), s32[]{:S(2)}) async-start(), calls=%async_computation.11 | async-start | bytes 2654208 | tf_op jit(solution)/shard_map/all_gather | solution.py:750
  53.9 395.7 %reduce-scatter.5.cloned.1.call-start = ((), (), s32[]{:S(2)}) async-start(), calls=%async_computation.4 | async-start | bytes 1327104 | tf_op jit(solution)/shard_map/reduce_scatter | solution.py:770
  386.3 129.6 %reduce-scatter.7.cloned.1.call-start = ((), (), s32[]{:S(2)}) async-start(), calls=%async_computation.5 | async-start | bytes 1327104 | tf_op jit(solution)/shard_map/reduce_scatter | solution.py:770
  386.9 206.6 %reduce-scatter.9.cloned.1.call-start = ((), (), s32[]{:S(2)}) async-start(), calls=%async_computation.6 | async-start | bytes 2654208 | tf_op jit(solution)/shard_map/reduce_scatter | solution.py:768
  387.7 277.7 %reduce-scatter.11.cloned.1.call-start = ((), (), s32[]{:S(2)}) async-start(), calls=%async_computation.7 | async-start | bytes 2654208 | tf_op jit(solution)/shard_map/reduce_scatter | solution.py:768
  517.1 13.0 %collective-permute-start.16 = (bf16[2,48,192]{2,1,0:T(8,128)(2,1)S(1)}, bf16[2,48,192]{2,1,0:T(8,128)(2,1)S(1)}, u32[]{:S(2)}, u32[]{:S(2)}) collective-permute-start(bf16[2,48,192]{2,1,0:T(8,128)(2,1)S(1)} %get-tuple-element.167), channel_id=1, source_target_pairs={{2,0},{4,1},{0,2},{6,3},{10,4},{12,5},{8,6},{14,7},{18,8},{20,9},{... | collective-permute-start | bytes 110600 | tf_op jit(solution)/shard_map/ppermute | solution.py:629
  520.6 17.5 %collective-permute-start.17 = (bf16[2,48,192]{2,1,0:T(8,128)(2,1)S(1)}, bf16[2,48,192]{2,1,0:T(8,128)(2,1)S(1)}, u32[]{:S(2)}, u32[]{:S(2)}) collective-permute-start(bf16[2,48,192]{2,1,0:T(8,128)(2,1)S(1)} %get-tuple-element.166), channel_id=1, source_target_pairs={{6,0},{0,1},{4,2},{2,3},{14,4},{8,5},{12,6},{10,7},{22,8},{16,9},{... | collective-permute-start | bytes 110600 | tf_op jit(solution)/shard_map/ppermute | solution.py:629
  521.6 17.9 %collective-permute-start.14 = (bf16[2,48,192]{2,1,0:T(8,128)(2,1)S(1)}, bf16[2,48,192]{2,1,0:T(8,128)(2,1)S(1)}, u32[]{:S(2)}, u32[]{:S(2)}) collective-permute-start(bf16[2,48,192]{2,1,0:T(8,128)(2,1)S(1)} %get-tuple-element.169), channel_id=1, source_target_pairs={{4,0},{0,1},{6,2},{2,3},{12,4},{8,5},{14,6},{10,7},{20,8},{16,9},{... | collective-permute-start | bytes 110600 | tf_op jit(solution)/shard_map/ppermute | solution.py:629
  522.7 18.2 %collective-permute-start.15 = (bf16[2,48,192]{2,1,0:T(8,128)(2,1)S(1)}, bf16[2,48,192]{2,1,0:T(8,128)(2,1)S(1)}, u32[]{:S(2)}, u32[]{:S(2)}) collective-permute-start(bf16[2,48,192]{2,1,0:T(8,128)(2,1)S(1)} %get-tuple-element.168), channel_id=1, source_target_pairs={{0,0},{4,1},{2,2},{6,3},{8,4},{12,5},{10,6},{14,7},{16,8},{20,9},{... | collective-permute-start | bytes 110600 | tf_op jit(solution)/shard_map/ppermute | solution.py:629
  523.3 17.6 %collective-permute-start.12 = (bf16[2,48,192]{2,1,0:T(8,128)(2,1)S(1)}, bf16[2,48,192]{2,1,0:T(8,128)(2,1)S(1)}, u32[]{:S(2)}, u32[]{:S(2)}) collective-permute-start(bf16[2,48,192]{2,1,0:T(8,128)(2,1)S(1)} %get-tuple-element.170), channel_id=1, source_target_pairs={{0,0},{6,1},{2,2},{4,3},{8,4},{14,5},{10,6},{12,7},{16,8},{22,9},{... | collective-permute-start | bytes 110600 | tf_op jit(solution)/shard_map/ppermute | solution.py:629
  530.1 10.8 %collective-permute-start.13 = (bf16[2,48,192]{2,1,0:T(8,128)(2,1)S(1)}, bf16[2,48,192]{2,1,0:T(8,128)(2,1)S(1)}, u32[]{:S(2)}, u32[]{:S(2)}) collective-permute-start(bf16[2,48,192]{2,1,0:T(8,128)(2,1)S(1)} %get-tuple-element.165), channel_id=1, source_target_pairs={{4,0},{2,1},{6,2},{0,3},{12,4},{10,5},{14,6},{8,7},{20,8},{18,9},{... | collective-permute-start | bytes 110600 | tf_op jit(solution)/shard_map/ppermute | solution.py:629
  538.1 130.3 %collective-permute-start.18 = (bf16[2,48,192]{2,1,0:T(8,128)(2,1)S(1)}, bf16[2,48,192]{2,1,0:T(8,128)(2,1)}, u32[]{:S(2)}, u32[]{:S(2)}) collective-permute-start(bf16[2,48,192]{2,1,0:T(8,128)(2,1)S(1)} %get-tuple-element.156), channel_id=1, source_target_pairs={{0,0},{4,1},{1,2},{5,3},{8,4},{12,5},{9,6},{13,7},{16,8},{20,9},{1... | collective-permute-start | bytes 110600 | tf_op jit(solution)/shard_map/ppermute | solution.py:629
  539.5 129.0 %collective-permute-start.19 = (bf16[2,48,192]{2,1,0:T(8,128)(2,1)S(1)}, bf16[2,48,192]{2,1,0:T(8,128)(2,1)}, u32[]{:S(2)}, u32[]{:S(2)}) collective-permute-start(bf16[2,48,192]{2,1,0:T(8,128)(2,1)S(1)} %get-tuple-element.155), channel_id=1, source_target_pairs={{4,0},{0,1},{5,2},{1,3},{12,4},{8,5},{13,6},{9,7},{20,8},{16,9},{2... | collective-permute-start | bytes 110600 | tf_op jit(solution)/shard_map/ppermute | solution.py:629
  711.5 18.2 %collective-permute-start.23 = (bf16[2,96,192]{2,1,0:T(8,128)(2,1)}, bf16[2,96,192]{2,1,0:T(8,128)(2,1)}, u32[]{:S(2)}, u32[]{:S(2)}) collective-permute-start(bf16[2,96,192]{2,1,0:T(8,128)(2,1)} %get-tuple-element.137), channel_id=1, source_target_pairs={{12,0},{0,1},{4,2},{8,3},{28,4},{16,5},{20,6},{24,7},{13,8},{1,9},... | collective-permute-start | bytes 221192 | tf_op jit(solution)/shard_map/ppermute | solution.py:629
  713.5 16.3 %collective-permute-start.22 = (bf16[2,96,192]{2,1,0:T(8,128)(2,1)}, bf16[2,96,192]{2,1,0:T(8,128)(2,1)}, u32[]{:S(2)}, u32[]{:S(2)}) collective-permute-start(bf16[2,96,192]{2,1,0:T(8,128)(2,1)} %get-tuple-element.136), channel_id=1, source_target_pairs={{8,0},{12,1},{0,2},{4,3},{24,4},{28,5},{16,6},{20,7},{9,8},{13,9},... | collective-permute-start | bytes 221192 | tf_op jit(solution)/shard_map/ppermute | solution.py:629
  715.8 14.0 %collective-permute-start.21 = (bf16[2,96,192]{2,1,0:T(8,128)(2,1)}, bf16[2,96,192]{2,1,0:T(8,128)(2,1)}, u32[]{:S(2)}, u32[]{:S(2)}) collective-permute-start(bf16[2,96,192]{2,1,0:T(8,128)(2,1)} %get-tuple-element.135), channel_id=1, source_target_pairs={{4,0},{8,1},{12,2},{0,3},{20,4},{24,5},{28,6},{16,7},{5,8},{9,9},{... | collective-permute-start | bytes 221192 | tf_op jit(solution)/shard_map/ppermute | solution.py:629
  719.5 10.3 %collective-permute-start.20 = (bf16[2,96,192]{2,1,0:T(8,128)(2,1)}, bf16[2,96,192]{2,1,0:T(8,128)(2,1)}, u32[]{:S(2)}, u32[]{:S(2)}) collective-permute-start(bf16[2,96,192]{2,1,0:T(8,128)(2,1)} %get-tuple-element.134), channel_id=1, source_target_pairs={{0,0},{4,1},{8,2},{12,3},{16,4},{20,5},{24,6},{28,7},{1,8},{5,9},{... | collective-permute-start | bytes 221192 | tf_op jit(solution)/shard_map/ppermute | solution.py:629
  (28 other events, 766.8 us)
Sparse Core Ops, SparseCore 0:
  34.5 48.6 all-gather.8
  86.0 51.0 all-gather.10
  139.9 39.5 all-gather.12
  182.1 50.8 all-gather.14
  386.4 63.1 reduce-scatter.4
  452.8 62.9 reduce-scatter.6
  519.4 74.0 reduce-scatter.8
  597.0 68.3 reduce-scatter.10

commit v2 on v1

--- a/solution.py
+++ b/solution.py
@@ -589,6 +589,721 @@
         ],
         3, 6, 10 << 30, (mg, h, wa, scales, tables, bias, *saved),
     )
+
+
+def feed_back_kernel(
+    g, mid, we_h, ws_h, sc, nb_h, act_h, slope_h, mid_grad, wg_o, rows_o,
+    we, ws, nb, act, slope, gl, hg, part, psend, precv, gown, gsend, grecv, lsem, ssem, rsem,
+):
+    d, x, c, peer, sib = place()
+    y = 1 - x
+    t = g.shape[0]
+    copies = Copies(lsem, ssem, rsem, d)
+    greet(d, peer, sib)
+    gl[x] = g[...].astype(BF)
+    g_sent = copies.push(gl.at[x], gl.at[x], peer)
+    we_own, ws_own = we.at[:, rows_of(c, D)], ws.at[rows_of(c, D), :]
+    weights = [
+        copies.local(ws_h, ws),
+        copies.local(we_h, we),
+        copies.local(slope_h, slope),
+        copies.local(act_h, act),
+        copies.local(nb_h, nb),
+    ]
+    for copy in weights:
+        copy.wait()
+
+    def back(block):
+        def step(i, carry):
+            lanes = pl.ds(pl.multiple_of(i * 256, 256), 256)
+            pulled = nt(gl[block], ws[lanes, :])
+            hg[block, :, lanes] = (pulled * slope[block, :, lanes].astype(F32)).astype(BF)
+            return carry
+
+        lax.fori_loop(0, HID // 256, step, 0)
+        return nt(hg[block], we[...])
+
+    part[...] = back(x)
+    g_sent.wait()
+    psend[...] = back(y).astype(BF)
+    part_sent = copies.push(psend, precv, peer)
+
+    gl_all = gl[...].reshape(2 * t, D)
+    nb_all = nb[...].reshape(2 * t, D)
+
+    def grads(which, store):
+        def step(i, carry):
+            at = pl.ds(pl.multiple_of(i * 256, 256), 256)
+            off = pl.ds(pl.multiple_of(which * D + i * 256, 256), 256)
+            hg_part = hg[:, :, off].reshape(2 * t, 256)
+            act_part = act[:, :, off].reshape(2 * t, 256)
+            store(0, at, tn(nb_all, hg_part))
+            store(1, at, tn(act_part, gl_all))
+            return carry
+
+        lax.fori_loop(0, D // 256, step, 0)
+
+    def to_send(kind, at, value):
+        if kind == 0:
+            gsend[:, at] = value.astype(BF)
+        else:
+            gsend[at, pl.ds(D, D)] = value.astype(BF)
+
+    def to_keep(kind, at, value):
+        if kind == 0:
+            gown[:, at] = value
+        else:
+            gown[at, pl.ds(D, D)] = value
+
+    grads(1 - c, to_send)
+    grad_sent = copies.push(gsend, grecv, sib)
+    grads(c, to_keep)
+    part_sent.wait()
+    dy = part[...] + precv[...].astype(F32)
+    back_mid, rows = norm_back(mid[...], sc[2:3, :], dy)
+    mid_grad[...] = g[...] + back_mid
+    rows_o[...] = rows
+    grad_sent.wait()
+    gsend[...] = (gown[...] + grecv[...].astype(F32)).astype(BF)
+    copies.local(gsend, wg_o).wait()
+
+
+def feed_back(g, mid, we, ws, scales, nb, act, slope):
+    t = g.shape[0]
+    return call(
+        feed_back_kernel, "feed_back", 5,
+        [vmem(), vmem(), hbm(), hbm(), vmem(), hbm(), hbm(), hbm()],
+        [vmem(), hbm(), vmem()],
+        [sds((t, D), F32), sds((D, 2 * D), BF), sds((2, D), F32)],
+        [
+            pltpu.VMEM((D, HID), BF), pltpu.VMEM((HID, D), BF), pltpu.VMEM((2, t, D), BF),
+            pltpu.VMEM((2, t, HID), BF), pltpu.VMEM((2, t, HID), BF), pltpu.VMEM((2, t, D), BF),
+            pltpu.VMEM((2, t, HID), BF), pltpu.VMEM((t, D), F32), pltpu.VMEM((t, D), BF),
+            pltpu.VMEM((t, D), BF), pltpu.VMEM((D, 2 * D), F32), pltpu.VMEM((D, 2 * D), BF),
+            pltpu.VMEM((D, 2 * D), BF),
+        ],
+        6, 3, 10 << 30, (g, mid, we, ws, scales, nb, act, slope),
+    )
+
+
+def attend_back_kernel(
+    mg, h, wt_h, wo_h, sc, cs, bias, na, q, k, v, ctx, lse, g_prev, wg_o, rows_o,
+    wt, wo, ml, cg, delta, dqt, dk, dv, kvsend, kvrecv, pg, part, psend, precv,
+    gown, gsend, grecv, lsem, ssem, rsem,
+):
+    d, x, c, peer, sib = place()
+    y = 1 - x
+    t = mg.shape[0]
+    copies = Copies(lsem, ssem, rsem, d)
+    greet(d, peer, sib)
+    ml[x] = mg[...].astype(BF)
+    ml_sent = copies.push(ml.at[x], ml.at[x], peer)
+    wt_own, wo_own = wt.at[rows_of(c, HALF), :], wo.at[:, rows_of(c, HALF)]
+    out_moves = [copies.local(wo_h, wo)]
+    tri_moves = [copies.local(wt_h, wt)]
+    dk[...] = jnp.zeros_like(dk)
+    dv[...] = jnp.zeros_like(dv)
+    for copy in out_moves:
+        copy.wait()
+
+    def attend(block):
+        other = 1 - block
+        pulled = nt(ml[block], wo[...])
+        cg[block] = pulled.astype(BF)
+        weighed = (cg[block].astype(F32) * ctx[block].astype(F32)).T
+        for head in range(HALF // HD):
+            delta[head : head + 1, :] = jnp.sum(
+                weighed[head * HD : head * HD + HD, :], axis=0, keepdims=True
+            )
+
+        def pair_step(p, carry):
+            lanes = pl.ds(pl.multiple_of(p * 128, 128), 128)
+            q_pair, cg_pair = q[block, :, lanes], cg[block, :, lanes]
+            for which in range(2):
+                q_head, cg_head = half_of(q_pair, which), half_of(cg_pair, which)
+                row = pl.ds(2 * p + which, 1)
+                total, dots = lse[block, row, :], delta[row, :]
+                turned = None
+                for side in (block, other):
+                    k_pair, v_pair = k[side, :, lanes], v[side, :, lanes]
+                    scores = nt(k_pair, q_head)
+                    if side is other:
+                        scores = scores + bias[0]
+                    probs = jnp.exp(scores - total)
+                    score_grad = (probs * (nt(v_pair, cg_head) - dots)).astype(BF)
+                    dv[side, :, lanes] += nn(probs.astype(BF), cg_head)
+                    dk[side, :, lanes] += nn(score_grad, q_head)
+                    piece = tn(k_pair, score_grad)
+                    turned = piece if turned is None else turned + piece
+                head = pl.ds(pl.multiple_of(p * 128 + which * HD, HD), HD)
+                dqt[block, head, :] = turned[which * HD : which * HD + HD, :] * HD**-0.5
+            return carry
+
+        lax.fori_loop(0, HALF // 128, pair_step, 0)
+
+    attend(x)
+    ml_sent.wait()
+    attend(y)
+    theirs, mine = rows_of(1 - c, t), rows_of(c, t)
+    for side in range(2):
+        kvsend[side, :, pl.ds(0, HALF)] = dk[side, theirs, :].astype(BF)
+        kvsend[side, :, pl.ds(HALF, HALF)] = dv[side, theirs, :].astype(BF)
+    kv_sent = copies.push(kvsend, kvrecv, sib)
+
+    def unturn(block, j, value):
+        cosine, sine = cs[block, :, 0:128], cs[block, :, 128:256]
+        rounded = value.astype(BF).astype(F32)
+        pg[block, :, pl.ds(128 * j, 128)] = turn(rounded, cosine, -sine).astype(BF)
+
+    for side in range(2):
+        for j in range(3):
+            unturn(side, j, dqt[side, 128 * j : 128 * j + 128, :].T)
+    kv_sent.wait()
+    for side in range(2):
+        for j in range(3):
+            at = pl.ds(128 * j, 128)
+            unturn(side, 3 + j, dk[side, mine, at] + kvrecv[side, :, at].astype(F32))
+            pg[side, :, pl.ds(D + 128 * j, 128)] = (
+                dv[side, mine, at] + kvrecv[side, :, pl.ds(HALF + 128 * j, 128)].astype(F32)
+            ).astype(BF)
+    for copy in tri_moves:
+        copy.wait()
+    psend[...] = nt(pg[y], wt[...]).astype(BF)
+    part_sent = copies.push(psend, precv, peer)
+    part[...] = nt(pg[x], wt[...])
+
+    ml_all = ml[...].reshape(2 * t, D)
+    na_all = na[...].reshape(2 * t, D)
+    ctx_all = ctx[...].reshape(2 * t, HALF)
+
+    def grads(which, store):
+        def step(i, carry):
+            off = pl.ds(pl.multiple_of(which * HALF + i * 128, 128), 128)
+            at = pl.ds(pl.multiple_of(i * 128, 128), 128)
+            store(0, at, tn(na[:, :, off].reshape(2 * t, 128), pg[...].reshape(2 * t, TRI)))
+            store(1, at, tn(ctx_all, ml[:, :, off].reshape(2 * t, 128)))
+            return carry
+
+        lax.fori_loop(0, HALF // 128, step, 0)
+
+    def to_send(kind, at, value):
+        if kind == 0:
+            gsend[at, pl.ds(0, TRI)] = value.astype(BF)
+        else:
+            gsend[:, pl.ds(pl.multiple_of(TRI + at.start, 128), 128)] = value.astype(BF)
+
+    def to_keep(kind, at, value):
+        if kind == 0:
+            gown[at, pl.ds(0, TRI)] = value
+        else:
+            gown[:, pl.ds(pl.multiple_of(TRI + at.start, 128), 128)] = value
+
+    grads(1 - c, to_send)
+    grad_sent = copies.push(gsend, grecv, sib)
+    grads(c, to_keep)
+    part_sent.wait()
+    dy = part[...] + precv[...].astype(F32)
+    back, rows = norm_back(h[...], sc[0:1, :], dy)
+    g_prev[...] = mg[...] + back
+    rows_o[...] = rows
+    grad_sent.wait()
+    gsend[...] = (gown[...] + grecv[...].astype(F32)).astype(BF)
+    copies.local(gsend, wg_o).wait()
+
+
+def attend_back(mg, h, wt, wo, scales, tables, bias, saved):
+    t = mg.shape[0]
+    return call(
+        attend_back_kernel, "attend_back", 6,
+        [vmem(), vmem(), hbm(), hbm(), vmem(), vmem(), pl.BlockSpec(memory_space=pltpu.SMEM)] + [vmem()] * 6,
+        [vmem(), hbm(), vmem()],
+        [sds((t, D), F32), sds((HALF, 2 * D), BF), sds((2, D), F32)],
+        [
+            pltpu.VMEM((D, TRI), BF), pltpu.VMEM((HALF, D), BF), pltpu.VMEM((2, t, D), BF),
+            pltpu.VMEM((2, t, HALF), BF), pltpu.VMEM((8, t), F32), pltpu.VMEM((2, HALF, t), F32),
+            pltpu.VMEM((2, 2 * t, HALF), F32), pltpu.VMEM((2, 2 * t, HALF), F32),
+            pltpu.VMEM((2, t, D), BF), pltpu.VMEM((2, t, D), BF), pltpu.VMEM((2, t, TRI), BF),
+            pltpu.VMEM((t, D), F32), pltpu.VMEM((t, D), BF), pltpu.VMEM((t, D), BF),
+            pltpu.VMEM((HALF, 2 * D), F32), pltpu.VMEM((HALF, 2 * D), BF),
+            pltpu.VMEM((HALF, 2 * D), BF),
+        ],
+        3, 4, 10 << 30, (mg, h, wt, wo, scales, tables, bias, *saved),
+    )
+
+
+KINDS = ("whole", "half", "out", "exp", "shr")
+
+
+class Refs:
+    def __init__(self, names, refs):
+        assert len(names) == len(refs)
+        for name, ref in zip(names, refs):
+            setattr(self, name, ref)
+
+
+def hold(ref):
+    return ref
+
+
+class Weights:
+    def __init__(self, n, dp, rows):
+        self.n = n
+        self.zs = dp // 2
+        self.rows = rows
+        s = lax.axis_index("seq")
+        self.s = s
+        self.x, self.c = lax.div(s, 2), lax.rem(s, 2)
+        self.d = lax.axis_index("dp")
+        self.z, self.y = lax.div(self.d, 2), lax.rem(self.d, 2)
+        self.sib, self.peer = s + 1 - 2 * self.c, lax.rem(s + 2, SEQ)
+        self.across = self.d + 1 - 2 * self.y
+        self.upper = lax.div(self.z, self.zs // 2)
+        self.source = {"whole": n.p_whole, "half": n.p_half, "out": n.p_out, "exp": n.p_exp, "shr": n.p_shr}
+
+    def slot(self, kind):
+        return self.z if kind == "exp" else 2 * lax.rem(self.z, self.zs // 2) + self.c
+
+    def target(self, kind):
+        if kind == "exp":
+            return self.s
+        if kind == "whole":
+            return 2 * self.x + self.upper
+        if kind == "half":
+            return 2 * (1 - self.x) + self.upper
+        return 2 * self.upper + self.x
+
+    def view(self, kind, layer, y, j, x, c):
+        n, r = self.n, self.rows
+        if kind == "exp":
+            return n.we.at[layer, rows_of(2 * j + y, r), rows_of(c, D)]
+        core = lax.rem(j, 2)
+        at = 2 * lax.div(j, 2) + y
+        if kind == "whole":
+            start = pl.multiple_of(HALF * c + r * at, r)
+            return n.wt.at[layer, pl.ds(start, r), rows_of(x + core, HALF)]
+        if kind == "half":
+            return n.hb.at[layer, core, rows_of(at, r), :]
+        if kind == "out":
+            return n.ob.at[layer, core, rows_of(at, r), :]
+        return n.sb.at[layer, core, rows_of(at, 4 * r), :]
+
+    def remote(self, src, dst, kind, layer, stage, sent, slot, to):
+        number = KINDS.index(kind)
+        return pltpu.make_async_remote_copy(
+            src_ref=src,
+            dst_ref=dst,
+            send_sem=self.n.ssem.at[layer, number, stage, sent],
+            recv_sem=self.n.rsem.at[layer, number, stage, slot],
+            device_id=to,
+            device_id_type=MESH,
+        )
+
+    def first(self, kind, layer, act):
+        number = KINDS.index(kind)
+        slot, to = self.slot(kind), self.target(kind)
+        src = self.source[kind].at[layer]
+        dst = self.view(kind, layer, self.y, slot, lax.div(to, 2), lax.rem(to, 2))
+
+        def one(k):
+            other = lax.rem(self.z + k, self.zs)
+            copy = self.remote(src, dst, kind, layer, 0, k, slot, (2 * other + self.y, to))
+            copy.start() if act == "start" else copy.wait_send()
+
+        def here():
+            if act == "start":
+                pltpu.make_async_copy(src, dst, self.n.rsem.at[layer, number, 0, slot]).start()
+
+        if kind == "exp":
+            here()
+        elif kind == "half":
+            one(0)
+        else:
+            pl.when(to == self.s)(here)
+            pl.when(to != self.s)(lambda: one(0))
+
+        def step(k, carry):
+            one(k)
+            return carry
+
+        lax.fori_loop(1, self.zs, step, 0)
+
+    def onward(self, kind, layer, j):
+        ref = self.view(kind, layer, self.y, j, self.x, self.c)
+        copy = self.remote(ref, ref, kind, layer, 0, j, j, (self.across, self.s))
+        copy.wait_recv()
+        self.remote(ref, ref, kind, layer, 1, j, j, (self.across, self.s)).start()
+
+    def onward_all(self, kind, layer):
+        def step(j, carry):
+            self.onward(kind, layer, j)
+            return carry
+
+        lax.fori_loop(0, self.zs, step, 0)
+
+    def arrive(self, kind, layer):
+        def step(j, carry):
+            ref = self.view(kind, layer, 1 - self.y, j, self.x, self.c)
+            self.remote(ref, ref, kind, layer, 1, j, j, (self.across, self.s)).wait_recv()
+            return carry
+
+        lax.fori_loop(0, self.zs, step, 0)
+
+    def finish(self, kind, layer):
+        self.first(kind, layer, "wait")
+
+        def step(j, carry):
+            ref = self.view(kind, layer, self.y, j, self.x, self.c)
+            self.remote(ref, ref, kind, layer, 1, j, j, (self.across, self.s)).wait_send()
+            return carry
+
+        lax.fori_loop(0, self.zs, step, 0)
+
+
+def greet_all(w):
+    barrier = pltpu.get_barrier_semaphore()
+
+    def one(i, carry):
+        z, s = lax.div(i, SEQ), lax.rem(i, SEQ)
+        away = jnp.logical_or(z != w.z, s != w.s)
+
+        @pl.when(away)
+        def _():
+            pl.semaphore_signal(barrier, inc=1, device_id=(2 * z + w.y, s), device_id_type=MESH)
+
+        return carry
+
+    lax.fori_loop(0, w.zs * SEQ, one, 0)
+    pl.semaphore_signal(barrier, inc=1, device_id=(w.across, w.s), device_id_type=MESH)
+    pl.semaphore_wait(barrier, w.zs * SEQ)
+
+
+def gather_scales_start(w):
+    n = w.n
+    mine = n.scl.at[w.y, w.z, w.s]
+    mine[...] = n.sc_own[...]
+
+    def one(i, carry):
+        z, s = lax.div(i, SEQ), lax.rem(i, SEQ)
+
+        @pl.when(jnp.logical_or(z != w.z, s != w.s))
+        def _():
+            pltpu.make_async_remote_copy(
+                src_ref=mine, dst_ref=mine, send_sem=n.sc_ssem.at[i],
+                recv_sem=n.sc_rsem.at[w.z * SEQ + w.s], device_id=(2 * z + w.y, s), device_id_type=MESH,
+            ).start()
+
+        return carry
+
+    lax.fori_loop(0, w.zs * SEQ, one, 0)
+
+
+def gather_scales_end(w):
+    n = w.n
+
+    def one(i, carry):
+        z, s = lax.div(i, SEQ), lax.rem(i, SEQ)
+
+        @pl.when(jnp.logical_or(z != w.z, s != w.s))
+        def _():
+            slot = n.scl.at[w.y, z, s]
+            copy = pltpu.make_async_remote_copy(
+                src_ref=slot, dst_ref=slot, send_sem=n.sc_ssem.at[i], recv_sem=n.sc_rsem.at[i],
+                device_id=(2 * z + w.y, s), device_id_type=MESH,
+            )
+            copy.wait_recv()
+            copy.wait_send()
+
+        return carry
+
+    lax.fori_loop(0, w.zs * SEQ, one, 0)
+    count = w.zs * SEQ
+    plane = n.scl.at[w.y]
+    copy = pltpu.make_async_remote_copy(
+        src_ref=plane, dst_ref=plane, send_sem=n.sc_ssem.at[count], recv_sem=n.sc_rsem.at[count],
+        device_id=(w.across, w.s), device_id_type=MESH,
+    )
+    copy.start()
+    copy.wait()
+    wide = n.sc.shape[-1] // (2 * w.zs)
+    for s in range(SEQ):
+        both = [n.scl[d % 2, d // 2, s][:, :wide] for d in range(2 * w.zs)]
+        rows = jnp.concatenate(both, axis=1)
+        for layer in range(LAYERS):
+            n.sc[layer, s : s + 1, :] = rows[layer : layer + 1, :]
+
+
+FWD_OUT = (
+    "h_out", "h_mid", "mid_o0", "mid_o1", "sc_o",
+    "na_o0", "q_o0", "k_o0", "v_o0", "ctx_o0", "lse_o0", "nb_o0", "act_o0", "slope_o0", "wt_o0", "wo_o0", "we_o0", "ws_o0",
+    "na_o1", "q_o1", "k_o1", "v_o1", "ctx_o1", "lse_o1", "nb_o1", "act_o1", "slope_o1", "wt_o1", "wo_o1", "we_o1", "ws_o1",
+)
+FWD_IN = ("h0", "sc_own", "cs", "bias", "p_whole", "p_half", "p_out", "p_exp", "p_shr")
+FWD_SCRATCH = (
+    "wt", "wo", "we", "ws", "hb", "ob", "sb", "scl", "sc", "na", "q", "k", "v", "ctxt", "ctx", "lse", "nb", "act",
+    "slope", "psend", "precv", "hs", "mid", "ssem", "rsem", "sc_ssem", "sc_rsem", "xs", "xr", "lsem",
+)
+
+
+def fwd_kernel(dp, *refs):
+    n = Refs((*FWD_IN, *FWD_OUT, *FWD_SCRATCH), refs)
+    rows = n.p_exp.shape[1]
+    t = n.h0.shape[0]
+    w = Weights(n, dp, rows)
+    x, c, peer, sib = w.x, w.c, w.peer, w.sib
+    y = 1 - x
+    copies = Copies(n.lsem, n.xs, n.xr, w.d)
+    waits = []
+
+    def save(src, dst):
+        waits.append(copies.local(src, dst))
+
+    greet_all(w)
+    w.first("whole", 0, "start")
+    w.first("half", 0, "start")
+    gather_scales_start(w)
+    w.first("out", 0, "start")
+    n.hs[0] = n.h0[...]
+    xhat, _ = norm_stats(n.hs[0])
+    gather_scales_end(w)
+
+    def share_tri(layer):
+        own = n.wt.at[layer, rows_of(c, HALF), :]
+        n.wt[layer, rows_of(c, HALF), rows_of(2 * (1 - x), HALF)] = jnp.concatenate(
+            [n.hb[layer, 0], n.hb[layer, 1]], axis=1
+        )
+        return copies.push(own, own, sib)
+
+    def share_cols(into, parts, layer):
+        own = into.at[layer, :, rows_of(c, HALF)]
+        into[layer, :, rows_of(c, HALF)] = jnp.concatenate([parts[layer, 0], parts[layer, 1]], axis=1)
+        return copies.push(own, own, sib)
+
+    def share_exp(layer):
+        own = n.we.at[layer, :, rows_of(c, D)]
+        return copies.push(own, own, sib)
+
+    for layer in range(LAYERS):
+        last = layer == LAYERS - 1
+        if layer:
+            xhat, _ = norm_stats(n.hs[layer])
+        n.na[layer, x] = (xhat * n.sc[layer, 0:1, :] + n.sc[layer, 1:2, :]).astype(BF)
+        na_sent = copies.push(n.na.at[layer, x], n.na.at[layer, x], peer)
+        if layer == 0:
+            w.onward_all("whole", 0)
+            w.onward_all("half", 0)
+            w.first("exp", 0, "start")
+            w.onward_all("out", 0)
+            w.first("shr", 0, "start")
+            w.arrive("whole", 0)
+            w.arrive("half", 0)
+            tri_sent = share_tri(0)
+        tri_sent.wait()
+
+        def project(block):
+            cosine, sine = n.cs[block, :, 0:128], n.cs[block, :, 128:256]
+            for j in range(9):
+                part = nn(n.na[layer, block], n.wt[layer, :, 128 * j : 128 * j + 128])
+                lanes = pl.ds(128 * (j % 3), 128)
+                if j < 3:
+                    n.q[layer, block, :, lanes] = (turn(part, cosine, sine) * HD**-0.5).astype(BF)
+                elif j < 6:
+                    n.k[layer, block, rows_of(c, t), lanes] = turn(part, cosine, sine).astype(BF)
+                else:
+                    n.v[layer, block, rows_of(c, t), lanes] = part.astype(BF)
+
+        def share(block):
+            at = (layer, block, rows_of(c, t))
+            return [
+                copies.push(n.k.at[at], n.k.at[at], sib),
+                copies.push(n.v.at[at], n.v.at[at], sib),
+            ]
+
+        project(x)
+        shared = share(x)
+        na_sent.wait()
+        project(y)
+        shared += share(y)
+        w.arrive("out", layer)
+        out_sent = share_cols(n.wo, n.ob, layer)
+        for copy in shared:
+            copy.wait()
+        save(n.na.at[layer], getattr(n, f"na_o{layer}"))
+        save(n.q.at[layer], getattr(n, f"q_o{layer}"))
+        save(n.k.at[layer], getattr(n, f"k_o{layer}"))
+        save(n.v.at[layer], getattr(n, f"v_o{layer}"))
+
+        def attend(block, pump):
+            other = 1 - block
+
+            def pair_step(p, carry):
+                pump(p)
+                lanes = pl.ds(pl.multiple_of(p * 128, 128), 128)
+                q_pair = n.q[layer, block, :, lanes]
+                k_same, k_cross = n.k[layer, block, :, lanes], n.k[layer, other, :, lanes]
+                v_same, v_cross = n.v[layer, block, :, lanes], n.v[layer, other, :, lanes]
+                for which in range(2):
+                    q_head = half_of(q_pair, which)
+                    s_same = nt(k_same, q_head)
+                    s_cross = nt(k_cross, q_head) + n.bias[0]
+                    top = jnp.maximum(
+                        jnp.max(s_same, axis=0, keepdims=True), jnp.max(s_cross, axis=0, keepdims=True)
+                    )
+                    e_same = jnp.exp(s_same - top)
+                    e_cross = jnp.exp(s_cross - top)
+                    total = jnp.sum(e_same, axis=0, keepdims=True) + jnp.sum(
+                        e_cross, axis=0, keepdims=True
+                    )
+                    mixed = tn(v_same, e_same.astype(BF)) + tn(v_cross, e_cross.astype(BF))
+                    head = pl.ds(pl.multiple_of(p * 128 + which * HD, HD), HD)
+                    n.ctxt[head, :] = mixed[which * HD : which * HD + HD, :] / total
+                    n.lse[layer, block, pl.ds(2 * p + which, 1), :] = top + jnp.log(total)
+                return carry
+
+            lax.fori_loop(0, HALF // 128, pair_step, 0)
+            n.ctx[layer, block] = n.ctxt[...].T.astype(BF)
+
+        attend(y, lambda p: w.onward("exp", layer, p))
+        out_sent.wait()
+        use = 2 * layer
+        n.psend[use] = nn(n.ctx[layer, y], n.wo[layer]).astype(BF)
+        part_sent = copies.push(n.psend.at[use], n.precv.at[use], peer)
+
+        def rest(p):
+            w.onward("shr", layer, p)
+
+        w.onward("exp", layer, w.zs - 1)
+        attend(x, rest)
+        w.onward("shr", layer, w.zs - 1)
+        if not last:
+            w.first("whole", layer + 1, "start")
+            w.first("half", layer + 1, "start")
+            w.first("out", layer + 1, "start")
+        n.mid[layer] = n.hs[layer] + nn(n.ctx[layer, x], n.wo[layer])
+        save(n.ctx.at[layer], getattr(n, f"ctx_o{layer}"))
+        save(n.lse.at[layer], getattr(n, f"lse_o{layer}"))
+        save(n.wt.at[layer], getattr(n, f"wt_o{layer}"))
+        save(n.wo.at[layer], getattr(n, f"wo_o{layer}"))
+        part_sent.wait()
+        n.mid[layer] = n.mid[layer] + n.precv[use].astype(F32)
+        save(n.mid.at[layer], getattr(n, f"mid_o{layer}"))
+
+        xhat, _ = norm_stats(n.mid[layer])
+        n.nb[layer, x] = (xhat * n.sc[layer, 2:3, :] + n.sc[layer, 3:4, :]).astype(BF)
+        nb_sent = copies.push(n.nb.at[layer, x], n.nb.at[layer, x], peer)
+        w.arrive("exp", layer)
+        exp_sent = share_exp(layer)
+        w.arrive("shr", layer)
+        shr_sent = share_cols(n.ws, n.sb, layer)
+        exp_sent.wait()
+
+        def feed(block, pump):
+            def step(i, carry):
+                pump(i)
+                lanes = pl.ds(pl.multiple_of(i * 256, 256), 256)
+                value, rate = gelu_parts(nn(n.nb[layer, block], n.we[layer, :, lanes]))
+                n.act[layer, block, :, lanes] = value.astype(BF)
+                n.slope[layer, block, :, lanes] = rate.astype(BF)
+                return carry
+
+            lax.fori_loop(0, HID // 256, step, 0)
+
+        def pump_tri(i):
+            if not last:
+
+                @pl.when(i < w.zs)
+                def _():
+                    w.onward("whole", layer + 1, i)
+                    w.onward("half", layer + 1, i)
+
+        def pump_out(i):
+            if not last:
+
+                @pl.when(i < w.zs)
+                def _():
+                    w.onward("out", layer + 1, i)
+
+        feed(x, pump_tri)
+        shr_sent.wait()
+        n.hs[layer + 1] = n.mid[layer] + nn(n.act[layer, x], n.ws[layer])
+        nb_sent.wait()
+        feed(y, pump_out)
+        use = 2 * layer + 1
+        n.psend[use] = nn(n.act[layer, y], n.ws[layer]).astype(BF)
+        part_sent = copies.push(n.psend.at[use], n.precv.at[use], peer)
+        save(n.nb.at[layer], getattr(n, f"nb_o{layer}"))
+        save(n.act.at[layer], getattr(n, f"act_o{layer}"))
+        save(n.slope.at[layer], getattr(n, f"slope_o{layer}"))
+        save(n.we.at[layer], getattr(n, f"we_o{layer}"))
+        save(n.ws.at[layer], getattr(n, f"ws_o{layer}"))
+        if not last:
+            w.first("exp", layer + 1, "start")
+            w.first("shr", layer + 1, "start")
+            w.arrive("whole", layer + 1)
+            w.arrive("half", layer + 1)
+            tri_sent = share_tri(layer + 1)
+        part_sent.wait()
+        n.hs[layer + 1] = n.hs[layer + 1] + n.precv[use].astype(F32)
+
+    n.h_out[...] = n.hs[LAYERS]
+    n.sc_o[...] = n.sc[...]
+    save(n.hs.at[1], n.h_mid)
+    for copy in waits:
+        copy.wait()
+    for layer in range(LAYERS):
+        for kind in KINDS:
+            w.finish(kind, layer)
+
+
+def forward_all(dp, h, sc_own, tables, bias, pieces):
+    t = h.shape[0]
+    zs = dp // 2
+    per_layer = [
+        sds((2, t, D), BF), sds((2, t, HALF), BF), sds((2, 2 * t, HALF), BF), sds((2, 2 * t, HALF), BF),
+        sds((2, t, HALF), BF), sds((2, 8, t), F32), sds((2, t, D), BF), sds((2, t, HID), BF), sds((2, t, HID), BF),
+        sds((D, TRI), BF), sds((HALF, D), BF), sds((D, HID), BF), sds((HID, D), BF),
+    ]
+    token = sds((t, D), F32)
+    outs = [token, token, token, token, sds((LAYERS, 4, D), F32), *per_layer, *per_layer]
+    specs = [vmem(), hbm(), hbm(), hbm(), vmem(), *([hbm()] * (2 * len(per_layer)))]
+    n_layers = LAYERS
+    scratch = [
+        pltpu.VMEM((n_layers, D, TRI), BF), pltpu.VMEM((n_layers, HALF, D), BF),
+        pltpu.VMEM((n_layers, D, HID), BF), pltpu.VMEM((n_layers, HID, D), BF),
+        pltpu.VMEM((n_layers, 2, HALF, 192), BF), pltpu.VMEM((n_layers, 2, HALF, 192), BF),
+        pltpu.VMEM((n_layers, 2, HID, 192), BF), pltpu.VMEM((2, zs, SEQ, 8, 128), F32),
+        pltpu.VMEM((n_layers, 4, D), F32), pltpu.VMEM((n_layers, 2, t, D), BF),
+        pltpu.VMEM((n_layers, 2, t, HALF), BF), pltpu.VMEM((n_layers, 2, 2 * t, HALF), BF),
+        pltpu.VMEM((n_layers, 2, 2 * t, HALF), BF), pltpu.VMEM((HALF, t), F32),
+        pltpu.VMEM((n_layers, 2, t, HALF), BF), pltpu.VMEM((n_layers, 2, 8, t), F32),
+        pltpu.VMEM((n_layers, 2, t, D), BF), pltpu.VMEM((n_layers, 2, t, HID), BF),
+        pltpu.VMEM((n_layers, 2, t, HID), BF), pltpu.VMEM((2 * n_layers, t, D), BF),
+        pltpu.VMEM((2 * n_layers, t, D), BF), pltpu.VMEM((n_layers + 1, t, D), F32),
+        pltpu.VMEM((n_layers, t, D), F32),
+        pltpu.SemaphoreType.DMA((n_layers, len(KINDS), 2, zs)),
+        pltpu.SemaphoreType.DMA((n_layers, len(KINDS), 2, zs)),
+        pltpu.SemaphoreType.DMA((zs * SEQ + 1,)), pltpu.SemaphoreType.DMA((zs * SEQ + 1,)),
+        pltpu.SemaphoreType.DMA((24,)), pltpu.SemaphoreType.DMA((24,)), pltpu.SemaphoreType.DMA((32,)),
+    ]
+    results = pl.pallas_call(
+        functools.partial(fwd_kernel, dp),
+        name="forward",
+        out_shape=outs,
+        in_specs=[vmem(), vmem(), vmem(), pl.BlockSpec(memory_space=pltpu.SMEM), *([hbm()] * 5)],
+        out_specs=specs,
+        scratch_shapes=scratch,
+        cost_estimate=pl.CostEstimate(flops=22 << 30, bytes_accessed=32 << 20, transcendentals=0),
+        compiler_params=pltpu.CompilerParams(
+            collective_id=4, has_side_effects=True, vmem_limit_bytes=VMEM_BYTES
+        ),
+    )(h, sc_own, tables, bias, *pieces)
+    return Refs(FWD_OUT, results)
+
+
+def pieces_of(triple_weight, output_weight, expand_weight, shrink_weight, c):
+    tri = triple_weight.astype(BF)
+    whole = jnp.where(c == 0, tri[:, :, :HALF], tri[:, :, 192:])
+    half = jnp.where(c == 0, tri[:, :, HALF:], tri[:, :, :192])
+    return whole, half, output_weight.astype(BF), expand_weight.astype(BF), shrink_weight.astype(BF)
 
 
 class Moves:
@@ -718,20 +1433,11 @@
     return tables, bias
 
 
-def local(dp, *args):
-    (residual, cotangent, segments) = args[:3]
-    (
-        triple_weight, triple_moment, triple_square, triple_shadow,
-        output_weight, output_moment, output_square, output_shadow,
-        expand_weight, expand_moment, expand_square, expand_shadow,
-        shrink_weight, shrink_moment, shrink_square, shrink_shadow,
-        scales_weight, scales_moment, scales_square, scales_shadow,
-    ) = args[3:]
-    moves = Moves(dp)
-    t = residual.shape[0]
+def layers_narrow(
+    dp, moves, residual, cotangent, scales_weight, tables, bias,
+    triple_weight, output_weight, expand_weight, shrink_weight,
+):
     d, s = lax.axis_index("dp"), lax.axis_index("seq")
-    tables, bias = tables_here(segments, t, moves.x, moves.c)
-
     scales_all = lax.psum(
         lax.dynamic_update_slice(
             jnp.zeros((LAYERS, 4, D), F32), scales_weight.astype(BF).astype(F32), (0, s, d * (D // dp))
@@ -770,6 +1476,56 @@
         attend_grads[layer] = scatter(attend_grad).astype(F32)
         scale_grads[layer] = jnp.concatenate([rows_a, rows_b], axis=0)
 
+    return stream, g, attend_grads, feed_grads, scale_grads
+
+
+def layers_wide(dp, residual, cotangent, sc_own, tables, bias, pieces):
+    f = forward_all(dp, residual, sc_own, tables, bias, pieces)
+    stream, scales_all = f.h_out, f.sc_o
+    g = cotangent
+    attend_grads, feed_grads, scale_grads = [None] * LAYERS, [None] * LAYERS, [None] * LAYERS
+    scatter = functools.partial(lax.psum_scatter, axis_name="dp", scatter_dimension=0, tiled=True)
+    for layer in reversed(range(LAYERS)):
+        scales = scales_all[layer]
+        h, middle = (f.h_mid, f.mid_o1) if layer else (residual, f.mid_o0)
+        feed_saved = [getattr(f, f"{k}_o{layer}") for k in ("nb", "act", "slope")]
+        attend_saved = [getattr(f, f"{k}_o{layer}") for k in ("na", "q", "k", "v", "ctx", "lse")]
+        wt, wo, we, ws = (getattr(f, f"{k}_o{layer}") for k in ("wt", "wo", "we", "ws"))
+        mg, feed_grad, rows_b = feed_back(g, middle, we, ws, scales, *feed_saved)
+        feed_grads[layer] = scatter(feed_grad).astype(F32)
+        g, attend_grad, rows_a = attend_back(mg, h, wt, wo, scales, tables, bias, attend_saved)
+        attend_grads[layer] = scatter(attend_grad).astype(F32)
+        scale_grads[layer] = jnp.concatenate([rows_a, rows_b], axis=0)
+    return stream, g, attend_grads, feed_grads, scale_grads
+
+
+def local(dp, *args):
+    (residual, cotangent, segments) = args[:3]
+    (
+        triple_weight, triple_moment, triple_square, triple_shadow,
+        output_weight, output_moment, output_square, output_shadow,
+        expand_weight, expand_moment, expand_square, expand_shadow,
+        shrink_weight, shrink_moment, shrink_square, shrink_shadow,
+        scales_weight, scales_moment, scales_square, scales_shadow,
+    ) = args[3:]
+    moves = Moves(dp)
+    t = residual.shape[0]
+    d, s = lax.axis_index("dp"), lax.axis_index("seq")
+    tables, bias = tables_here(segments, t, moves.x, moves.c)
+
+    if (D // dp) % 16 == 0:
+        sc_own = jnp.zeros((8, 128), F32)
+        sc_own = sc_own.at[:LAYERS, : D // dp].set(scales_weight[:, 0].astype(BF).astype(F32))
+        pieces = pieces_of(triple_weight, output_weight, expand_weight, shrink_weight, moves.c)
+        stream, g, attend_grads, feed_grads, scale_grads = layers_wide(
+            dp, residual, cotangent, sc_own, tables, bias, pieces
+        )
+    else:
+        stream, g, attend_grads, feed_grads, scale_grads = layers_narrow(
+            dp, moves, residual, cotangent, scales_weight, tables, bias,
+            triple_weight, output_weight, expand_weight, shrink_weight,
+        )
+
     scale_grad = lax.psum(jnp.stack(scale_grads), ("dp", "seq"))
     own_scale = lax.dynamic_slice(scale_grad, (0, s, d * (D // dp)), (LAYERS, 1, D // dp))
     squares = jnp.sum(own_scale * own_scale)

time: 754 us -> 687 us (0.911)
  Pallas kernels: 242 us -> 297 us
  blocking collectives: 133 us -> 79.4 us
  waiting for transfers between devices: 249 us -> 205 us
  starting transfers between devices: 60.9 us -> 30.5 us
    pallas_call x0 -> x1, Pallas kernels: none -> 170 us  [forward_all(): pl.pallas_call(functools.partial(fwd_kernel, dp), name='forward', out_sha...]
    pallas_call x8 -> x4, Pallas kernels: 242 us -> 127 us  [call(): pl.pallas_call(kernel, name=name, out_shape=out_shape, in_specs=ins, out_...]
    psum x1 -> x0, blocking collectives: 53.8 us -> none  [local(): lax.psum(lax.dynamic_update_slice(jnp.zeros((LAYERS, 4, D), F32), scales_...]
    all_gather x4 -> x0, waiting for transfers between devices: 31.2 us -> none  [the longest x2 22.4 us: local(): wf.append(gather(feed_parts[layer]))]
    ppermute x24 -> x12, starting transfers between devices: 60.6 us -> 30.4 us  [send(): return lax.ppermute(piece, ('dp', 'seq'), perm)]
  transfers between devices with their start and end apart: 32 -> 16, of which waited for: 9 -> 4; matrix products, arithmetic and copies ran while one was open for 3% -> 3% of each run, Pallas kernels for 12% -> 0%
where the time goes in v2:
time: 687 us; the launch traced here: 674 us
  Pallas kernels  297 us (43%)
  waiting for transfers between devices  205 us (30%)
  blocking collectives  79.4 us (12%)
  other arithmetic  32.7 us (5%)
  starting transfers between devices  30.5 us (4%)
  between operations  21.9 us (3%)
  local copies, waits for them, and re-layouts  7.88 us (1%)
    pallas_call x1, Pallas kernels, forward_all(): pl.pallas_call(functools.partial(fwd_kernel, dp), name='forward', out_sha...  170 us
    pallas_call x4, Pallas kernels, call(): pl.pallas_call(kernel, name=name, out_shape=out_shape, in_specs=ins, out_...  127 us
    reduce_scatter x2, waiting for transfers between devices, layers_wide(): feed_grads[layer] = scatter(feed_grad).astype(F32)  116 us
    reduce_scatter x2, waiting for transfers between devices, layers_wide(): attend_grads[layer] = scatter(attend_grad).astype(F32)  86.9 us
    psum x1, blocking collectives, local(): scale_grad = lax.psum(jnp.stack(scale_grads), ('dp', 'seq'))  40 us
    psum x1, blocking collectives, local(): grad_norm = jnp.sqrt(lax.psum(squares, ('dp', 'seq')))  39.4 us
    ppermute x12, starting transfers between devices, send(): return lax.ppermute(piece, ('dp', 'seq'), perm)  30.4 us
  transfers between devices with their start and end apart: 16, of which 4 were waited for; matrix products, arithmetic and copies ran while one was open for 3% of the time, Pallas kernels for 0%

profile of v2, /device:TPU:0, one launch (start us, length us, event | category | flops | bytes accessed | tf_op | source)
XLA Modules:
  0.0 673.8 jit_solution(9724778234418512329)
XLA Ops:
  9.9 1.3 fusion.37
  17.4 169.6 %forward.1 = (f32[256,768]{1,0:T(8,128)}, f32[256,768]{1,0:T(8,128)}, f32[256,768]{1,0:T(8,128)}, f32[256,768]{1,0:T(8,128)}, f32[2,4,768]{2,1,0:T(4,128)}, /*in...) custom-call(f32[256,768]{1,0:T(8,128)} %h.1, ...), custom_call_target="tpu_custom_call" | custom-call | flops 23622320128 | bytes 33554432 | tf_op jit(solution)/shard_map/forward/pallas_call | solution.py:1287
  188.3 28.4 %feed_back.2 = (f32[256,768]{1,0:T(8,128)}, bf16[768,1536]{1,0:T(8,128)(2,1)}, f32[2,768]{1,0:T(2,128)}) custom-call(f32[256,768]{1,0:T(8,128)} %g.1, f32[256,768]{1,0:T(8,128)} %get-tuple-element.79.mid, bf16[768,1536]{1,0:T(8,128)(2,1)} %get-tuple-element.80.we_h, bf16[1536,768]{1,0:T(8,128)(2,1)} %get-tuple-element.81.ws_h, ...), custom_call_target="tpu_custom_call" | custom-call | flops 10737418240 | bytes 16777216 | tf_op jit(solution)/shard_map/feed_back/pallas_call | solution.py:240
  216.8 35.4 %attend_back.2 = (f32[256,768]{1,0:T(8,128)}, bf16[384,1536]{1,0:T(8,128)(2,1)}, f32[2,768]{1,0:T(2,128)}) custom-call(f32[256,768]{1,0:T(8,128)} %get-tuple-element.86.mg, f32[256,768]{1,0:T(8,128)} %get-tuple-element.87.h, bf16[768,1152]{1,0:T(8,128)(2,1)} %get-tuple-element.88.wt_h, bf16[384,768]{1,0:T(8,128)(2,1)} %get-tuple-element.89.wo_h, ...), custom_call_target="tpu_custom_call" | custom-call | flops 10737418240 | bytes 16777216 | tf_op jit(solution)/shard_map/attend_back/pallas_call | solution.py:240
  252.1 27.9 %feed_back.3 = (f32[256,768]{1,0:T(8,128)}, bf16[768,1536]{1,0:T(8,128)(2,1)}, f32[2,768]{1,0:T(2,128)}) custom-call(f32[256,768]{1,0:T(8,128)} %get-tuple-element.96.g, f32[256,768]{1,0:T(8,128)} %get-tuple-element.97.mid, bf16[768,1536]{1,0:T(8,128)(2,1)} %get-tuple-element.98.we_h, bf16[1536,768]{1,0:T(8,128)(2,1)} %get-tuple-element.99.ws_h, ...), custom_call_target="tpu_custom_call" | custom-call | flops 10737418240 | bytes 16777216 | tf_op jit(solution)/shard_map/feed_back/pallas_call | solution.py:240
  280.0 35.4 %attend_back.3 = (f32[256,768]{1,0:T(8,128)}, bf16[384,1536]{1,0:T(8,128)(2,1)}, f32[2,768]{1,0:T(2,128)}) custom-call(f32[256,768]{1,0:T(8,128)} %get-tuple-element.103.mg, f32[256,768]{1,0:T(8,128)} %h.1, bf16[768,1152]{1,0:T(8,128)(2,1)} %get-tuple-element.104.wt_h, bf16[384,768]{1,0:T(8,128)(2,1)} %get-tuple-element.105.wo_h, ...), custom_call_target="tpu_custom_call" | custom-call | flops 10737418240 | bytes 16777216 | tf_op jit(solution)/shard_map/attend_back/pallas_call | solution.py:240
  318.2 40.0 %psum.14 = f32[2,4,768]{2,1,0:T(4,128)S(1)} all-reduce(f32[2,4,768]{2,1,0:T(4,128)S(1)} %pad_maximum_fusion.4), channel_id=1, replica_groups=mesh['dp'=8,'seq'=4] {'dp','seq'}, use_global_device_ids=true, to_apply=%region_0.1 | all-reduce | flops 6144 | bytes 49152 | tf_op jit(solution)/shard_map/psum | solution.py:1529
  358.8 20.5 %reduce-scatter.5.cloned.1.call-done = bf16[48,1536]{1,0:T(8,128)(2,1)} async-done(((bf16[384,1536]{1,0:T(8,128)(2,1)}), bf16[48,1536]{1,0:T(8,128)(2,1)}) %reduce-scatter.5.cloned.1.call-update) | async-done | bytes 147472 | tf_op jit(solution)/shard_map/reduce_scatter | solution.py:1497
  379.3 66.5 %reduce-scatter.7.cloned.1.call-done = bf16[48,1536]{1,0:T(8,128)(2,1)} async-done(((bf16[384,1536]{1,0:T(8,128)(2,1)}), bf16[48,1536]{1,0:T(8,128)(2,1)}) %reduce-scatter.7.cloned.1.call-update) | async-done | bytes 147472 | tf_op jit(solution)/shard_map/reduce_scatter | solution.py:1497
  447.4 2.8 collective-permute-start.7
  452.1 2.0 collective-permute-start.1
  455.3 2.2 collective-permute-start.2
  457.5 1.6 multiply_reduce_fusion.3
  459.1 1.6 multiply_reduce_fusion.2
  463.3 4.2 collective-permute-start.4
  468.2 4.8 collective-permute-start.5
  473.9 1.5 fusion.22
  475.4 46.4 %reduce-scatter.9.cloned.1.call-done = bf16[96,1536]{1,0:T(8,128)(2,1)} async-done(((bf16[768,1536]{1,0:T(8,128)(2,1)}), bf16[96,1536]{1,0:T(8,128)(2,1)}) %reduce-scatter.9.cloned.1.call-update) | async-done | bytes 294928 | tf_op jit(solution)/shard_map/reduce_scatter | solution.py:1495
  521.8 1.8 multiply_reduce_fusion.1
  523.6 69.4 %reduce-scatter.11.cloned.1.call-done = bf16[96,1536]{1,0:T(8,128)(2,1)} async-done(((bf16[768,1536]{1,0:T(8,128)(2,1)}), bf16[96,1536]{1,0:T(8,128)(2,1)}) %reduce-scatter.11.cloned.1.call-update) | async-done | bytes 294928 | tf_op jit(solution)/shard_map/reduce_scatter | solution.py:1495
  593.0 1.7 multiply_reduce_fusion
  596.1 1.5 fusion.18
  597.6 39.4 %psum.15 = f32[]{:T(128)} all-reduce(f32[]{:T(128)S(6)} %add.389), channel_id=1, replica_groups=mesh['dp'=8,'seq'=4] {'dp','seq'}, use_global_device_ids=true, to_apply=%region_10.11 | all-reduce | flops 1 | bytes 8 | tf_op jit(solution)/shard_map/psum | solution.py:1534
  637.7 2.0 fusion.8
  639.7 2.1 collective-permute-start.8
  641.9 4.9 collective-permute-start.9
  646.8 2.5 collective-permute-start.10
  649.3 2.2 collective-permute-start.11
  651.8 2.9 multiply_add_fusion.2
  656.3 1.7 multiply_add_fusion.4
  658.0 1.5 multiply_add_fusion.8
  661.2 2.1 multiply_add_fusion
  (124 shorter events, 24.0 us)
Async XLA Ops:
  7.2 4.0 copy-start.2
  7.2 5.0 copy-start.1
  7.2 372.1 %reduce-scatter.5.cloned.1.call-start = ((), (), s32[]{:S(2)}) async-start(), calls=%async_computation.4 | async-start | bytes 1327104 | tf_op jit(solution)/shard_map/reduce_scatter | solution.py:1497
  8.4 4.5 copy-start.4
  8.4 5.2 copy-start.30
  315.5 130.3 %reduce-scatter.7.cloned.1.call-start = ((), (), s32[]{:S(2)}) async-start(), calls=%async_computation.5 | async-start | bytes 1327104 | tf_op jit(solution)/shard_map/reduce_scatter | solution.py:1497
  316.2 205.6 %reduce-scatter.9.cloned.1.call-start = ((), (), s32[]{:S(2)}) async-start(), calls=%async_computation.6 | async-start | bytes 2654208 | tf_op jit(solution)/shard_map/reduce_scatter | solution.py:1495
  317.0 276.0 %reduce-scatter.11.cloned.1.call-start = ((), (), s32[]{:S(2)}) async-start(), calls=%async_computation.7 | async-start | bytes 2654208 | tf_op jit(solution)/shard_map/reduce_scatter | solution.py:1495
  358.1 92.1 %copy-start.25 = (f32[2,4,768]{2,1,0:T(4,128)}, f32[2,4,768]{2,1,0:T(4,128)S(1)}, u32[]{:S(2)}) copy-start(f32[2,4,768]{2,1,0:T(4,128)S(1)} %psum.14) | copy-start | bytes 73732
  446.7 15.9 %collective-permute-start.6 = (bf16[2,48,192]{2,1,0:T(8,128)(2,1)S(1)}, bf16[2,48,192]{2,1,0:T(8,128)(2,1)S(1)}, u32[]{:S(2)}, u32[]{:S(2)}) collective-permute-start(bf16[2,48,192]{2,1,0:T(8,128)(2,1)S(1)} %get-tuple-element.173), channel_id=1, source_target_pairs={{0,0},{4,1},{1,2},{5,3},{8,4},{12,5},{9,6},{13,7},{16,8},{20,9},{1... | collective-permute-start | bytes 110600 | tf_op jit(solution)/shard_map/ppermute | solution.py:1344
  447.4 15.9 %collective-permute-start.7 = (bf16[2,48,192]{2,1,0:T(8,128)(2,1)S(1)}, bf16[2,48,192]{2,1,0:T(8,128)(2,1)S(1)}, u32[]{:S(2)}, u32[]{:S(2)}) collective-permute-start(bf16[2,48,192]{2,1,0:T(8,128)(2,1)S(1)} %get-tuple-element.172), channel_id=1, source_target_pairs={{4,0},{0,1},{5,2},{1,3},{12,4},{8,5},{13,6},{9,7},{20,8},{16,9},{2... | collective-permute-start | bytes 110600 | tf_op jit(solution)/shard_map/ppermute | solution.py:1344
  451.2 200.4 %copy-start.7 = (f32[2,96,768]{2,1,0:T(8,128)S(1)}, f32[2,96,768]{2,1,0:T(8,128)}, u32[]{:S(2)}) copy-start(f32[2,96,768]{2,1,0:T(8,128)} %param.39) | copy-start | bytes 1769476
  451.2 200.4 %copy-start.8 = (f32[2,96,768]{2,1,0:T(8,128)S(1)}, f32[2,96,768]{2,1,0:T(8,128)}, u32[]{:S(2)}) copy-start(f32[2,96,768]{2,1,0:T(8,128)} %param.37) | copy-start | bytes 1769476
  451.2 200.4 %copy-start.9 = (f32[2,96,768]{2,1,0:T(8,128)S(1)}, f32[2,96,768]{2,1,0:T(8,128)}, u32[]{:S(2)}) copy-start(f32[2,96,768]{2,1,0:T(8,128)} %param.38) | copy-start | bytes 1769476
  452.1 16.2 %collective-permute-start.1 = (bf16[2,48,192]{2,1,0:T(8,128)(2,1)S(1)}, bf16[2,48,192]{2,1,0:T(8,128)(2,1)}, u32[]{:S(2)}, u32[]{:S(2)}) collective-permute-start(bf16[2,48,192]{2,1,0:T(8,128)(2,1)S(1)} %get-tuple-element.174), channel_id=1, source_target_pairs={{4,0},{2,1},{6,2},{0,3},{12,4},{10,5},{14,6},{8,7},{20,8},{18,9},{... | collective-permute-start | bytes 110600 | tf_op jit(solution)/shard_map/ppermute | solution.py:1344
  454.1 19.0 %collective-permute-start = (bf16[2,48,192]{2,1,0:T(8,128)(2,1)S(1)}, bf16[2,48,192]{2,1,0:T(8,128)(2,1)}, u32[]{:S(2)}, u32[]{:S(2)}) collective-permute-start(bf16[2,48,192]{2,1,0:T(8,128)(2,1)S(1)} %get-tuple-element.179), channel_id=1, source_target_pairs={{0,0},{6,1},{2,2},{4,3},{8,4},{14,5},{10,6},{12,7},{16,8},{22,9},{... | collective-permute-start | bytes 110600 | tf_op jit(solution)/shard_map/ppermute | solution.py:1344
  455.3 18.6 %collective-permute-start.2 = (bf16[2,48,192]{2,1,0:T(8,128)(2,1)S(1)}, bf16[2,48,192]{2,1,0:T(8,128)(2,1)}, u32[]{:S(2)}, u32[]{:S(2)}) collective-permute-start(bf16[2,48,192]{2,1,0:T(8,128)(2,1)S(1)} %get-tuple-element.178), channel_id=1, source_target_pairs={{4,0},{0,1},{6,2},{2,3},{12,4},{8,5},{14,6},{10,7},{20,8},{16,9},{... | collective-permute-start | bytes 110600 | tf_op jit(solution)/shard_map/ppermute | solution.py:1344
  462.7 11.2 %collective-permute-start.3 = (bf16[2,48,192]{2,1,0:T(8,128)(2,1)S(1)}, bf16[2,48,192]{2,1,0:T(8,128)(2,1)S(1)}, u32[]{:S(2)}, u32[]{:S(2)}) collective-permute-start(bf16[2,48,192]{2,1,0:T(8,128)(2,1)S(1)} %get-tuple-element.177), channel_id=1, source_target_pairs={{0,0},{4,1},{2,2},{6,3},{8,4},{12,5},{10,6},{14,7},{16,8},{20,9},{... | collective-permute-start | bytes 110600 | tf_op jit(solution)/shard_map/ppermute | solution.py:1344
  463.3 132.7 %collective-permute-start.4 = (bf16[2,48,192]{2,1,0:T(8,128)(2,1)}, bf16[2,48,192]{2,1,0:T(8,128)(2,1)}, u32[]{:S(2)}, u32[]{:S(2)}) collective-permute-start(bf16[2,48,192]{2,1,0:T(8,128)(2,1)} %get-tuple-element.176), channel_id=1, source_target_pairs={{2,0},{4,1},{0,2},{6,3},{10,4},{12,5},{8,6},{14,7},{18,8},{20,9},{... | collective-permute-start | bytes 110600 | tf_op jit(solution)/shard_map/ppermute | solution.py:1344
  468.2 127.8 %collective-permute-start.5 = (bf16[2,48,192]{2,1,0:T(8,128)(2,1)}, bf16[2,48,192]{2,1,0:T(8,128)(2,1)}, u32[]{:S(2)}, u32[]{:S(2)}) collective-permute-start(bf16[2,48,192]{2,1,0:T(8,128)(2,1)} %get-tuple-element.175), channel_id=1, source_target_pairs={{6,0},{0,1},{4,2},{2,3},{14,4},{8,5},{12,6},{10,7},{22,8},{16,9},{... | collective-permute-start | bytes 110600 | tf_op jit(solution)/shard_map/ppermute | solution.py:1344
  521.8 129.8 %copy-start = (bf16[96,1536]{1,0:T(8,128)(2,1)S(1)}, bf16[96,1536]{1,0:T(8,128)(2,1)}, u32[]{:S(2)}) copy-start(bf16[96,1536]{1,0:T(8,128)(2,1)} %reduce-scatter.9.cloned.1.call-done) | copy-start | bytes 884740
  639.7 19.8 %collective-permute-start.8 = (bf16[2,96,192]{2,1,0:T(8,128)(2,1)}, bf16[2,96,192]{2,1,0:T(8,128)(2,1)}, u32[]{:S(2)}, u32[]{:S(2)}) collective-permute-start(bf16[2,96,192]{2,1,0:T(8,128)(2,1)} %get-tuple-element.164), channel_id=1, source_target_pairs={{0,0},{4,1},{8,2},{12,3},{16,4},{20,5},{24,6},{28,7},{1,8},{5,9},{... | collective-permute-start | bytes 221192 | tf_op jit(solution)/shard_map/ppermute | solution.py:1344
  641.9 17.6 %collective-permute-start.9 = (bf16[2,96,192]{2,1,0:T(8,128)(2,1)}, bf16[2,96,192]{2,1,0:T(8,128)(2,1)}, u32[]{:S(2)}, u32[]{:S(2)}) collective-permute-start(bf16[2,96,192]{2,1,0:T(8,128)(2,1)} %get-tuple-element.165), channel_id=1, source_target_pairs={{4,0},{8,1},{12,2},{0,3},{20,4},{24,5},{28,6},{16,7},{5,8},{9,9},{... | collective-permute-start | bytes 221192 | tf_op jit(solution)/shard_map/ppermute | solution.py:1344
  646.8 12.7 %collective-permute-start.10 = (bf16[2,96,192]{2,1,0:T(8,128)(2,1)}, bf16[2,96,192]{2,1,0:T(8,128)(2,1)}, u32[]{:S(2)}, u32[]{:S(2)}) collective-permute-start(bf16[2,96,192]{2,1,0:T(8,128)(2,1)} %get-tuple-element.166), channel_id=1, source_target_pairs={{8,0},{12,1},{0,2},{4,3},{24,4},{28,5},{16,6},{20,7},{9,8},{13,9},... | collective-permute-start | bytes 221192 | tf_op jit(solution)/shard_map/ppermute | solution.py:1344
  649.3 10.2 %collective-permute-start.11 = (bf16[2,96,192]{2,1,0:T(8,128)(2,1)}, bf16[2,96,192]{2,1,0:T(8,128)(2,1)}, u32[]{:S(2)}, u32[]{:S(2)}) collective-permute-start(bf16[2,96,192]{2,1,0:T(8,128)(2,1)} %get-tuple-element.167), channel_id=1, source_target_pairs={{12,0},{0,1},{4,2},{8,3},{28,4},{16,5},{20,6},{24,7},{13,8},{1,9},... | collective-permute-start | bytes 221192 | tf_op jit(solution)/shard_map/ppermute | solution.py:1344
  651.7 4.0 copy-start.15
  651.7 4.0 copy-start.16
  651.7 4.0 copy-start.17
  651.7 4.0 copy-start.18
  651.8 4.0 copy-start.19
  658.0 3.2 copy-start.10
  658.0 3.2 copy-start.11
  (18 other events, 35.6 us)
Sparse Core Ops, SparseCore 0:
  315.6 63.6 reduce-scatter.4
  382.7 63.0 reduce-scatter.6
  449.3 72.4 reduce-scatter.8
  525.1 67.8 reduce-scatter.10
